TPU v7x, 32 devices: a whole 2x2x4 slice. The times are simulated.
32 devices in a mesh: replica: 8 (over z, x), brick: 4 (over y, core).
Axes of the slice: x: 2, y: 2, z: 4, core: 2. Of those that a mesh axis runs over, the one named last changes fastest.
Arguments:
- atom_locations: float32 [8, 3, 3072], P('replica', None, 'brick'), may hold values from 0 to 128, as said below
- atom_speeds_vector: float32 [8, 3, 3072], P('replica', None, 'brick'), may hold values from -7 to 7
- inertial_amounts: float32 [3072], P('brick'), may hold values from 1 to 4
- electric_loads: float32 [3072], P('brick'), may hold values from -4 to 4
- scatter_strengths: float32 [3072], P('brick'), may hold values from 0.5 to 2
- gaussian_spreads_sigma: float32 [3072], P('brick'), may hold values from 0.7 to 1.4
- atom_present_flags: int32 [3072], P('brick'), may hold values 0 or 1
- observed_volume_values: float32 [40, 128, 128], P('brick'), may hold values from 0 to 2
- voxel_reciprocal_spread: float32 [40, 128, 128], P('brick'), may hold values from 0.5 to 4
- paired_partner_lists: int32 [24, 14], P('brick'), may hold values from 0 to 9
- cell_usage_tally: int32 [24], P('brick'), may hold values from 1 to 14, as said below
- halo_sender_spots: int32 [2, 1024], P(None, 'brick'), may hold values from 0 to 767
- target_warmth_levels: int32 [8], P('replica'), may hold values from 280 to 399
Outputs:
- new_positions: float32 [8, 3, 3072], P('replica', None, 'brick')
- new_velocities: float32 [8, 3, 3072], P('replica', None, 'brick')
- deviation: float32 [40, 128, 128], P('brick', 'replica')
Inputs may be any that keep to these rules, and one draw needn't show every extreme that they name: `atom_locations`: atoms in the slots of brick b have x in [b * 10, (b + 1) * 10), y in [0, 128), z in [0, 128). Only the first cell_usage_tally[c] slots of cell c count; some cell uses all 14 slots.
All inputs are finite; a program needn't handle non-finite values. No bound on the sum of `atom_present_flags` on one device may be relied on, other than what follows from the above.
Results may differ from a plain program's by a relative error of at most 0.00062.
Values may be sent and summed in bfloat16 or wider, within the bound.
No kernel may reach another device: no remote copies, remote signals or barrier semaphores. Data moves between devices by JAX's collectives and lax.ppermute only.
A program may use at most 64 MiB of HBM per device.

v0:
```python
import functools
import math

import jax
import jax.numpy as jnp
from jax import lax
from jax.experimental import pallas as pl
from jax.experimental.pallas import tpu as pltpu
from jax.sharding import PartitionSpec as P

HALO = 2
CELL = 128
RIM = 2 * HALO

restraint = 0.1
coupling = 5.0
softening = 1.0
timestep = 0.5
boltzmann = 0.015
heat_bath_damping = 0.5

F32 = jnp.float32
BF16 = jnp.bfloat16
NT = (((1,), (1,)), ((), ()))
VMEM = pl.BlockSpec(memory_space=pltpu.VMEM)
SMEM = pl.BlockSpec(memory_space=pltpu.SMEM)
HBM = pl.BlockSpec(memory_space=pltpu.HBM)


def bell(grid, coord, rate, period=None):
    delta = grid - coord
    if period is not None:
        away = jnp.abs(delta)
        delta = jnp.minimum(away, period - away)
    return jnp.exp2(delta * delta * rate)


def bell_slope(grid, coord, inv_var, rate, period=None):
    delta = grid - coord
    if period is not None:
        delta = delta - period * jnp.floor(delta * (1.0 / period) + 0.5)
    value = jnp.exp2(delta * delta * rate)
    return value, delta * inv_var * value


def limit(mib):
    return pltpu.CompilerParams(vmem_limit_bytes=mib << 20)


def in_hbm(x):
    return pltpu.with_memory_space_constraint(x, pltpu.HBM)


def cost(us):
    return pl.CostEstimate(flops=us * 500_000_000, bytes_accessed=us * 1_000_000, transcendentals=0)


def iota(shape, dim):
    return lax.broadcasted_iota(jnp.int32, shape, dim)


def row_class(rows, members):
    share = rows // members
    bit = 0
    while (share << bit) % 8:
        bit += 1
    return share, bit, share << bit


def local_rows(shape, member, bit, block):
    row = iota(shape, 0)
    own = (member >> bit) & 1
    return ((row // block) * (2 * block) + own * block + row % block).astype(F32)


def prep_kernel(
    coords, speeds, flags, scatter, loads, sigma, mass, spots, lists, live, obs, weight,
    mine, speed_out, par, plan, up, down, obs_out, weight_out,
    flags_s, floats_s, spots_s, lists_s, live_s, small_sem, sem, row_sem, *, thick, bit, half,
):
    own = (lax.axis_index("replica") >> bit) & 1
    block = obs.shape[3]
    small = [
        pltpu.make_async_copy(flags, flags_s.at[0], small_sem.at[0]),
        pltpu.make_async_copy(spots, spots_s, small_sem.at[1]),
        pltpu.make_async_copy(coords, mine.at[0], small_sem.at[6]),
        pltpu.make_async_copy(speeds, speed_out, small_sem.at[9]),
        pltpu.make_async_copy(lists, lists_s, small_sem.at[7]),
        pltpu.make_async_copy(live, live_s, small_sem.at[8]),
    ]
    for n, source in enumerate((scatter, loads, sigma, mass)):
        small.append(pltpu.make_async_copy(source, floats_s.at[n, 0], small_sem.at[2 + n]))
    for copy in small:
        copy.start()
    copies = []
    deals = half // block
    for target, first in ((up, thick - HALO), (down, 0)):
        for n, source in enumerate((obs, weight)):
            for plane in range(HALO):
                copies.append(
                    pltpu.make_async_copy(
                        source.at[first + plane, :, own],
                        target.at[pl.ds((n * HALO + plane) * deals, deals)],
                        sem.at[len(copies)],
                    )
                )
                copies[-1].start()
    for source, target in ((obs, obs_out), (weight, weight_out)):
        for q in range(deals):
            copies.append(
                pltpu.make_async_copy(
                    source.at[:, q, own],
                    target.at[:, pl.ds(q * block, block)],
                    row_sem.at[len(copies) - 4 * HALO],
                )
            )
            copies[-1].start()
    for copy in small:
        copy.wait()
    occupancy = flags_s[...].astype(F32)
    inv_var = 1.0 / (floats_s[2] * floats_s[2])
    charge = occupancy * floats_s[1]
    par[0:1] = occupancy * floats_s[0]
    par[1:2] = charge
    par[2:3] = inv_var
    par[3:4] = (-0.5 * math.log2(math.e)) * inv_var
    par[4:5] = floats_s[3]
    data = jnp.concatenate([mine[0, 0], mine[0, 1], mine[0, 2], charge], 0)
    high = data.astype(BF16)
    rest = data - high.astype(F32)
    mid = rest.astype(BF16)
    low = (rest - mid.astype(F32)).astype(BF16)
    pieces = jnp.concatenate([high.astype(F32), mid.astype(F32), low.astype(F32)], 0).astype(BF16)
    count = data.shape[1]
    cells, slots = lists_s.shape
    lane, row = iota((8, CELL), 1), iota((8, CELL), 0)
    used = jnp.zeros((8, CELL), jnp.int32)
    for c in range(cells):
        used = jnp.where(row == c, live_s[c], used)
    listed = jnp.concatenate([lists_s[...], jnp.zeros((8 - cells, slots), jnp.int32)], 0)
    picked = [jnp.zeros((8, CELL), jnp.int32)] * 2
    length = [jnp.zeros((8, CELL), jnp.int32)] * 2
    for s in range(slots):
        block_of = jnp.broadcast_to(listed[:, s : s + 1], (8, CELL))
        for kind in range(2):
            takes = (s < used) & ((block_of < cells) if kind == 0 else (block_of >= cells))
            picked[kind] = jnp.where(takes & (lane == length[kind]), block_of - kind * cells, picked[kind])
            length[kind] = length[kind] + takes.astype(jnp.int32)
    for kind in range(2):
        plan[kind] = jnp.where(lane == COUNT_AT, length[kind], picked[kind])
    for side, target in enumerate((up, down)):
        chosen = spots_s[side : side + 1, :]
        pick = (iota((count, chosen.shape[1]), 0) == chosen).astype(F32).astype(BF16)
        got = jnp.dot(pieces, pick, preferred_element_type=F32)
        got = got[0:4] + got[4:8] + got[8:12]
        groups = chosen.shape[1] // CELL
        for n in range(4):
            for g in range(groups):
                row = n * groups + g
                target[2 * HALO * deals, row : row + 1, :] = got[
                    n : n + 1, g * CELL : (g + 1) * CELL
                ]
    for copy in copies:
        copy.wait()


def spread_grids(half, depth, count, thick, bit, block):
    first = lax.axis_index("brick") * thick - HALO
    x_grid = (iota((16, count), 0) + first).astype(F32)
    y_grid = local_rows((half, count), lax.axis_index("replica"), bit, block)
    z_grid = iota((depth, count), 0).astype(F32)
    return x_grid, y_grid, z_grid


def member_bells(place, amp, rate, grids):
    x_grid, y_grid, z_grid = grids
    x_amp = amp * bell(x_grid, place[0], rate)
    y_val = bell(y_grid, place[1], rate, 2 * y_grid.shape[0])
    z_val = bell(z_grid, place[2], rate, z_grid.shape[0]).astype(BF16)
    return x_amp, y_val, z_val


def layers(left, x_amp, y_val, planes):
    half = y_val.shape[0]
    for n, i in enumerate(planes):
        left[n * half : (n + 1) * half, :] = (x_amp[i : i + 1] * y_val).astype(BF16)


def product(left, z_val, shape):
    return lax.dot_general(left[...], z_val, NT, preferred_element_type=F32).reshape(shape)


def early_kernel(*refs, thick, bit, block):
    groups, par, out, lefts, deeps = refs[:-6], refs[-6], refs[-5], refs[-4:-2], refs[-2:]
    planes, half, depth = out.shape
    count = par.shape[1]
    amp, rate = par[0:1], par[3:4]
    grids = spread_grids(half, depth, count, thick, bit, block)
    places = [(g, n) for g in groups for n in range(g.shape[0])]

    def build(m):
        g, n = places[m]
        x_amp, y_val, z_val = member_bells(g.at[n], amp, rate, grids)
        deeps[m % 2][...] = z_val
        layers(lefts[m % 2], x_amp, y_val, range(planes))

    build(0)
    for m in range(len(places)):
        if m + 1 < len(places):
            build(m + 1)
        got = product(lefts[m % 2], deeps[m % 2][...], out.shape)
        out[...] = got if m == 0 else out[...] + got


def rim_side(across, thick):
    odd = lax.axis_index("brick") % 2
    return thick * (odd if across else 1 - odd)


def pack_rim(rim, packet, base):
    packet[:RIM] = rim[...].astype(BF16)
    exact = rim[pl.ds(jnp.where(base == 0, 0, HALO), HALO)]
    packet[RIM:] = (exact - exact.astype(BF16).astype(F32)).astype(BF16)


def unpack_rim(packet, n, low):
    value = packet[n].astype(F32)
    extra = n - HALO if low else n
    return value + packet[RIM + extra].astype(F32) if 0 <= extra < HALO else value


def rim_bells(base, place, amp, rate, thick):
    first = lax.axis_index("brick") * thick - HALO + base
    grid = (iota((8, amp.shape[1]), 0) + first).astype(F32)
    return amp * bell(grid, place[0], rate)


def across_kernel(late, par, total, out, packet, x_out, y_out, z_out, left_a, left_b, *, thick, bit, block):
    members = late.shape[0]
    _, half, depth = total.shape
    amp, rate = par[0:1], par[3:4]
    grids = spread_grids(half, depth, par.shape[1], thick, bit, block)
    lefts = (left_a, left_b)
    base = rim_side(True, thick)

    def build(m):
        x_amp, y_val, z_val = member_bells(late.at[m], amp, rate, grids)
        x_out[m], y_out[m], z_out[m] = x_amp, y_val, z_val
        layers(lefts[m % 2], rim_bells(base, late.at[m], amp, rate, thick), y_val, range(RIM))

    build(0)
    for m in range(members):
        if m + 1 < members:
            build(m + 1)
        got = product(lefts[m % 2], z_out[m], out.shape)
        out[...] = got + (total[pl.ds(base, RIM)] if m == 0 else out[...])
    pack_rim(out, packet, base)


def beside_kernel(late, par, total, y_in, z_in, out, packet, left_a, left_b, *, thick):
    members = late.shape[0]
    amp, rate = par[0:1], par[3:4]
    lefts = (left_a, left_b)
    base = rim_side(False, thick)

    def build(m):
        layers(lefts[m % 2], rim_bells(base, late.at[m], amp, rate, thick), y_in[m], range(RIM))

    build(0)
    for m in range(members):
        if m + 1 < members:
            build(m + 1)
        got = product(lefts[m % 2], z_in[m], out.shape)
        out[...] = got + (total[pl.ds(base, RIM)] if m == 0 else out[...])
    pack_rim(out, packet, base)


FIXED = float(2**25)


def fixed(v):
    whole = jnp.floor(v)
    return (whole.astype(jnp.int32) << 25) + ((v - whole) * FIXED).astype(jnp.int32)


def enter(tables, n, x, y, z, q):
    at = slice(n * CELL, (n + 1) * CELL)
    for table, row in zip(tables, (x * FIXED, fixed(y), fixed(z), q)):
        table[at, :] = jnp.broadcast_to(row, (CELL, CELL)).T


def ghost_kernel(low, high, *tables, n_x, ghosts):
    slabs = lax.axis_size("brick")
    brick = lax.axis_index("brick")
    last = low.shape[0] - 1
    shift_low = jnp.where(brick == 0, -float(n_x), 0.0).astype(F32)
    shift_high = jnp.where(brick == slabs - 1, float(n_x), 0.0).astype(F32)
    for n, (ref, shift) in enumerate(((low, shift_low), (high, shift_high))):
        for g in range(ghosts):
            row = [ref[last, k * ghosts + g : k * ghosts + g + 1, :] for k in range(4)]
            enter(tables, n * ghosts + g, row[0] + shift, row[1], row[2], row[3])


def own_kernel(mine, par, plan, *refs):
    tables, (out, plan_s, sem) = refs[:4], refs[4:]
    copy = pltpu.make_async_copy(plan, plan_s, sem)
    copy.start()
    for c in range(mine.shape[3] // CELL):
        at = slice(c * CELL, (c + 1) * CELL)
        enter(tables, c, mine[0, 0, :, at], mine[0, 1, :, at], mine[0, 2, :, at], par[1:2, at])
    copy.wait()
    pair_cells(mine, par, [tables], [0], plan_s, out, 0)


COUNT_AT = 127


def pair_cells(mine, par, kinds, which, plan, out, first):
    for c in range(first, first + out.shape[1] // CELL):
        at = slice(c * CELL, (c + 1) * CELL)
        xi = jnp.broadcast_to(mine[0, 0, :, at] * FIXED, (8, CELL))
        yi = jnp.broadcast_to(fixed(mine[0, 1, :, at]), (8, CELL))
        zi = jnp.broadcast_to(fixed(mine[0, 2, :, at]), (8, CELL))
        zero = jnp.zeros((8, CELL), F32)
        total = (zero, zero, zero)
        for kind, tables in zip(which, kinds):
            place_x, place_y, place_z, load = tables

            def slot(s, total):
                start = pl.multiple_of(plan[kind, c, s] * CELL, CELL)
                tx, ty, tz = total
                for g in range(CELL // 8):
                    here = pl.ds(start + g * 8, 8)
                    dx = xi - place_x[here, :]
                    dy = (yi - place_y[here, :]).astype(F32)
                    dz = (zi - place_z[here, :]).astype(F32)
                    dist = dx * dx + dy * dy + (dz * dz + softening * FIXED * FIXED)
                    inv = lax.rsqrt(dist)
                    w = load[here, :] * inv * (inv * inv)
                    tx, ty, tz = tx + w * dx, ty + w * dy, tz + w * dz
                return tx, ty, tz

            def two_slots(n, total):
                return slot(2 * n + 1, slot(2 * n, total))

            slots = plan[kind, c, COUNT_AT]
            total = lax.fori_loop(0, slots // 2, two_slots, total)
            total = lax.fori_loop(2 * (slots // 2), slots, slot, total)
        factor = (coupling * FIXED * FIXED) * par[1:2, at]
        here = slice((c - first) * CELL, (c - first + 1) * CELL)
        for k in range(3):
            out[k : k + 1, here] = factor * jnp.sum(total[k], axis=0, keepdims=True)


def middle_kernel(
    late, x_in, y_in, z_in, total, mine, par, plan, obs, weight, *refs, thick, bit, block, members
):
    ghosts, (dev_out, grad, partner_out, short, left_a, left_b, plan_s, sem) = refs[:4], refs[4:]
    copy = pltpu.make_async_copy(plan, plan_s, sem)
    copy.start()
    planes = range(RIM, thick)
    lefts = (left_a, left_b)
    held = x_in.shape[0]
    half = total.shape[1]
    layers(left_a, x_in[0], y_in[0], planes)
    for m in range(held):
        if m + 1 < held:
            layers(lefts[(m + 1) % 2], x_in[m + 1], y_in[m + 1], planes)
        got = product(lefts[m % 2], z_in[m], dev_out.shape)
        dev_out[...] = got + (total[RIM:thick] if m == 0 else dev_out[...])
    for n, i in enumerate(planes):
        dev = dev_out[n] / members - obs[i - HALO]
        dev_out[n] = dev
        grad[n * half : (n + 1) * half, :] = (restraint * weight[i - HALO] * dev).astype(BF16)
    member_force(
        late.at[0], par, grad, partner_out,
        planes=planes, half=half, thick=thick, bit=bit, block=block,
    )
    copy.wait()
    pair_cells(mine, par, [ghosts], [1], plan_s, short, 0)


def member_force(place, par, grad, out, *, planes, half, thick, bit, block, plus=None):
    count = par.shape[1]
    depth = grad.shape[1]
    x_grid, y_grid, z_grid = spread_grids(half, depth, CELL, thick, bit, block)
    for t in range(count // CELL):
        at = slice(t * CELL, (t + 1) * CELL)
        inv_var, rate = par[2:3, at], par[3:4, at]
        x_val, x_der = bell_slope(x_grid, place[0, :, at], inv_var, rate)
        y_val, y_der = bell_slope(y_grid, place[1, :, at], inv_var, rate, 2 * half)
        z_val, z_der = bell_slope(z_grid, place[2, :, at], inv_var, rate, depth)
        z_pair = jnp.concatenate([z_val, z_der], 1).astype(BF16)
        got = jnp.dot(grad[...], z_pair, preferred_element_type=F32)
        sums = [jnp.zeros((8, CELL), F32) for _ in range(3)]
        for n, i in enumerate(planes):
            part = [jnp.zeros((8, CELL), F32) for _ in range(3)]
            for g in range(half // 8):
                j = slice(g * 8, (g + 1) * 8)
                k = slice(n * half + g * 8, n * half + (g + 1) * 8)
                along, across = got[k, :CELL], got[k, CELL:]
                part[0] += y_val[j] * along
                part[1] += y_der[j] * along
                part[2] += y_val[j] * across
            sums[0] += x_der[i : i + 1] * part[0]
            sums[1] += x_val[i : i + 1] * part[1]
            sums[2] += x_val[i : i + 1] * part[2]
        for k in range(3):
            force = -par[0:1, at] * jnp.sum(sums[k], axis=0, keepdims=True)
            out[k : k + 1, at] = force if plus is None else force + plus[k : k + 1, at]


def grad_kernel(
    late, par, sent_y, got_y, sent_c, got_c, dev_middle, grad_middle, partner_middle,
    near_low, near_high, obs, weight,
    dev_out, grad, partner_out, grad_rim, dev_s, *, thick, bit, share, block, members,
):
    _, half, _ = dev_middle.shape
    deals = near_low.shape[0] // (2 * HALO)
    member = lax.axis_index("replica")

    def near_rows(ref, n, plane):
        at = (n * HALO + plane) * deals
        return jnp.concatenate([ref[at + q] for q in range(deals)], 0)

    even = lax.axis_index("brick") % 2 == 0
    rims = [*range(RIM), *range(thick, thick + RIM)]
    for at, i in enumerate(rims):
        low, n = i < RIM, at % RIM
        across = sent_y[n] + unpack_rim(got_y, n, low)
        beside = sent_c[n] + unpack_rim(got_c, n, low)
        summed = jnp.where(even == low, across, beside)
        if i < HALO:
            wanted, trust = near_rows(near_low, 0, i), near_rows(near_low, 1, i)
        elif i >= thick + HALO:
            beyond = i - thick - HALO
            wanted, trust = near_rows(near_high, 0, beyond), near_rows(near_high, 1, beyond)
        else:
            wanted, trust = obs[i - HALO], weight[i - HALO]
        dev = summed / members - wanted
        slope = (restraint * trust * dev).astype(BF16)
        grad_rim[at * half : (at + 1) * half, :] = slope
        grad[i * half : (i + 1) * half, :] = slope
        if HALO <= i < thick + HALO:
            dev_s[i - HALO] = dev
    grad[RIM * half : thick * half, :] = grad_middle[...]
    dev_s[RIM - HALO : thick - HALO] = dev_middle[...]
    first_row = member * share
    spot = (first_row // (2 * block)) * block + first_row % block
    for n in range(half // share):

        @pl.when(spot == n * share)
        def _(n=n):
            dev_out[...] = dev_s[:, n * share : (n + 1) * share, :]

    member_force(
        late.at[0], par, grad_rim, partner_out,
        planes=rims, half=half, thick=thick, bit=bit, block=block, plus=partner_middle,
    )


def force_kernel(grad, mine, par, plan, *refs, thick, bit, block, first):
    own, (out, short, plan_s, sem) = refs[:4], refs[4:]
    copy = pltpu.make_async_copy(plan, plan_s, sem)
    copy.start()
    planes = range(thick + 2 * HALO)
    half = grad.shape[0] // len(planes)
    member_force(
        mine.at[0], par, grad, out, planes=planes, half=half, thick=thick, bit=bit, block=block
    )
    copy.wait()
    pair_cells(mine, par, [own], [0], plan_s, short, first)


def kick_kernel(own, other, short_own, short_a, short_b, par, speed, v_half, part):
    mass = par[4:5]
    energy = jnp.zeros_like(mass)
    for k in range(3):
        short = jnp.concatenate([short_own[k : k + 1], short_b[k : k + 1]], 1)
        short = short + short_a[k : k + 1]
        force = own[k : k + 1] + other[k : k + 1] + short
        v = speed[k] + timestep * force / mass
        v_half[k : k + 1] = v
        energy = energy + mass * v * v
    part[...] = jnp.broadcast_to(jnp.sum(energy, axis=1, keepdims=True), part.shape)


def drift_kernel(*refs, freedom):
    parts, (v_half, coords, warmth, place_out, speed_out) = refs[:-5], refs[-5:]
    kinetic = parts[0][0:1]
    for part in parts[1:]:
        kinetic = kinetic + part[0:1]
    present_moment = kinetic / (freedom * boltzmann) + 1e-06
    ratio = jnp.sqrt(
        1.0 + heat_bath_damping * (warmth[0].astype(F32) / present_moment - 1.0)
    )
    ratio = jnp.concatenate([ratio] * (v_half.shape[1] // ratio.shape[1]), 1)
    for k in range(3):
        v = ratio * v_half[k : k + 1]
        speed_out[k] = v
        place_out[k] = coords[0, k] + timestep * v


def local(
    atom_locations,
    atom_speeds_vector,
    inertial_amounts,
    electric_loads,
    scatter_strengths,
    gaussian_spreads_sigma,
    atom_present_flags,
    observed_volume_values,
    voxel_reciprocal_spread,
    paired_partner_lists,
    cell_usage_tally,
    halo_sender_spots,
    target_warmth_levels,
):
    thick, rows, depth = observed_volume_values.shape
    slabs = lax.axis_size("brick")
    members = lax.axis_size("replica")
    n_x = thick * slabs
    coords = jnp.transpose(atom_locations, (1, 0, 2))
    speeds = jnp.transpose(atom_speeds_vector, (1, 0, 2))
    count = coords.shape[2]
    planes = thick + 2 * HALO
    share, bit, block = row_class(rows, members)
    half = rows // 2
    deals = half // block
    ghosts = halo_sender_spots.shape[1]
    assert 4 * ghosts // CELL <= block
    assert slabs >= 4 and slabs % 2 == 0 and thick >= RIM and count // CELL <= 8

    bits = [1 << n for n in range(members.bit_length() - 1) if n != bit][::-1]

    def hop(known, mask):
        return lax.ppermute(known, "replica", [(i, i ^ mask) for i in range(members)])

    first = hop(coords[None], bits[0])
    obs = in_hbm(observed_volume_values.reshape(thick, deals, 2, block, depth))
    weight = in_hbm(voxel_reciprocal_spread.reshape(thick, deals, 2, block, depth))
    near = jax.ShapeDtypeStruct((2 * HALO * deals + 1, block, CELL), F32)
    own_rows = jax.ShapeDtypeStruct((thick, half, depth), F32)
    mine, speed, par, plan, near_up, near_down, own_obs, own_weight = pl.pallas_call(
        functools.partial(prep_kernel, thick=thick, bit=bit, half=half),
        out_shape=(
            jax.ShapeDtypeStruct((1,) + coords.shape, F32),
            jax.ShapeDtypeStruct(speeds.shape, F32),
            jax.ShapeDtypeStruct((8, count), F32),
            jax.ShapeDtypeStruct((2, 8, CELL), jnp.int32),
            near,
            near,
            own_rows,
            own_rows,
        ),
        in_specs=[HBM] * 12,
        out_specs=(VMEM,) * 8,
        scratch_shapes=[
            pltpu.VMEM((1, count), jnp.int32),
            pltpu.VMEM((4, 1, count), F32),
            pltpu.VMEM((2, ghosts), jnp.int32),
            pltpu.VMEM(paired_partner_lists.shape, jnp.int32),
            pltpu.SMEM(cell_usage_tally.shape, jnp.int32),
            pltpu.SemaphoreType.DMA((10,)),
            pltpu.SemaphoreType.DMA((4 * HALO,)),
            pltpu.SemaphoreType.DMA((2 * deals,)),
        ],
        compiler_params=limit(4),
        cost_estimate=cost(1),
        name="prep",
    )(
        *(
            in_hbm(a)
            for a in (
                coords,
                speeds,
                atom_present_flags,
                scatter_strengths,
                electric_loads,
                gaussian_spreads_sigma,
                inertial_amounts,
                halo_sender_spots,
                paired_partner_lists,
                cell_usage_tally,
            )
        ),
        obs,
        weight,
    )
    groups = [mine, first]
    for mask in bits[1:]:
        groups.append(hop(jnp.concatenate(groups), mask))
    late = hop(jnp.concatenate(groups), 1 << bit)

    ring = [(i, (i + 1) % slabs) for i in range(slabs)]
    back = [(target, source) for source, target in ring]
    near_low = lax.ppermute(near_up, "brick", ring)
    near_high = lax.ppermute(near_down, "brick", back)

    cells = count // CELL
    now = 2 * cells // 3

    def tables(blocks):
        table = jax.ShapeDtypeStruct((blocks * CELL, CELL), F32)
        table_int = jax.ShapeDtypeStruct((blocks * CELL, CELL), jnp.int32)
        return table, table_int, table_int, table

    planned = [pltpu.SMEM(plan.shape, jnp.int32), pltpu.SemaphoreType.DMA]
    *own_tables, short_own = pl.pallas_call(
        own_kernel,
        out_shape=(*tables(cells), jax.ShapeDtypeStruct((3, now * CELL), F32)),
        in_specs=[VMEM] * 3,
        out_specs=(VMEM,) * 5,
        scratch_shapes=planned,
        compiler_params=limit(6),
        cost_estimate=cost(2),
        name="own_pairs",
    )(mine, par, plan)
    ghost_tables = pl.pallas_call(
        functools.partial(ghost_kernel, n_x=n_x, ghosts=ghosts // CELL),
        out_shape=tables(2 * ghosts // CELL),
        in_specs=[VMEM] * 2,
        out_specs=(VMEM,) * 4,
        compiler_params=limit(6),
        cost_estimate=cost(1),
        name="ghosts",
    )(near_low, near_high)

    place = dict(thick=thick, bit=bit, block=block)
    total = pl.pallas_call(
        functools.partial(early_kernel, **place),
        out_shape=jax.ShapeDtypeStruct((planes, half, depth), F32),
        in_specs=[VMEM] * (len(groups) + 1),
        out_specs=VMEM,
        scratch_shapes=[pltpu.VMEM((planes * half, count), BF16)] * 2
        + [pltpu.VMEM((depth, count), BF16)] * 2,
        compiler_params=limit(12),
        cost_estimate=cost(2),
        name="early",
    )(*groups, par)
    held = late.shape[0]
    rim = jax.ShapeDtypeStruct((RIM, half, depth), F32)
    packet = jax.ShapeDtypeStruct((RIM + HALO, half, depth), BF16)
    sent_y, packet_y, x_late, y_late, z_late = pl.pallas_call(
        functools.partial(across_kernel, **place),
        out_shape=(
            rim,
            packet,
            jax.ShapeDtypeStruct((held, 16, count), F32),
            jax.ShapeDtypeStruct((held, half, count), F32),
            jax.ShapeDtypeStruct((held, depth, count), BF16),
        ),
        in_specs=[VMEM] * 3,
        out_specs=(VMEM,) * 5,
        scratch_shapes=[pltpu.VMEM((RIM * half, count), BF16)] * 2,
        compiler_params=limit(12),
        cost_estimate=cost(1),
        name="across",
    )(late, par, total)
    route = [(i, (i + 1 if i % 2 else i - 1) % slabs) for i in range(slabs)]
    got_y = lax.ppermute(packet_y, "brick", route)
    sent_c, packet_c = pl.pallas_call(
        functools.partial(beside_kernel, thick=thick),
        out_shape=(rim, packet),
        in_specs=[VMEM] * 5,
        out_specs=(VMEM, VMEM),
        scratch_shapes=[pltpu.VMEM((RIM * half, count), BF16)] * 2,
        compiler_params=limit(12),
        cost_estimate=cost(1),
        name="beside",
    )(late, par, total, y_late, z_late)
    got_c = lax.ppermute(packet_c, "brick", [(i, i ^ 1) for i in range(slabs)])
    force = jax.ShapeDtypeStruct((3, count), F32)
    inner = thick - RIM
    dev_middle, grad_middle, partner_middle, short_a = pl.pallas_call(
        functools.partial(middle_kernel, **place, members=members),
        out_shape=(
            jax.ShapeDtypeStruct((inner, half, depth), F32),
            jax.ShapeDtypeStruct((inner * half, depth), BF16),
            force,
            force,
        ),
        in_specs=[VMEM] * 14,
        out_specs=(VMEM,) * 4,
        scratch_shapes=[pltpu.VMEM((inner * half, count), BF16)] * 2 + planned,
        compiler_params=limit(12),
        cost_estimate=cost(2),
        name="middle",
    )(late, x_late, y_late, z_late, total, mine, par, plan, own_obs, own_weight, *ghost_tables)
    deviation, grad, partner = pl.pallas_call(
        functools.partial(grad_kernel, **place, share=share, members=members),
        out_shape=(
            jax.ShapeDtypeStruct((thick, share, depth), F32),
            jax.ShapeDtypeStruct((planes * half, depth), BF16),
            force,
        ),
        in_specs=[VMEM] * 13,
        out_specs=(VMEM, VMEM, VMEM),
        scratch_shapes=[
            pltpu.VMEM((2 * RIM * half, depth), BF16),
            pltpu.VMEM((thick, half, depth), F32),
        ],
        compiler_params=limit(12),
        cost_estimate=cost(1),
        name="grad",
    )(
        late, par, sent_y, got_y, sent_c, got_c, dev_middle, grad_middle, partner_middle,
        near_low, near_high, own_obs, own_weight,
    )

    swap = [(i, i ^ (1 << bit)) for i in range(members)]
    other = lax.ppermute(partner, "replica", swap)
    own, short_b = pl.pallas_call(
        functools.partial(force_kernel, **place, first=now),
        out_shape=(force, jax.ShapeDtypeStruct((3, count - now * CELL), F32)),
        in_specs=[VMEM] * 8,
        out_specs=(VMEM, VMEM),
        scratch_shapes=planned,
        compiler_params=limit(8),
        cost_estimate=cost(2),
        name="force",
    )(grad, mine, par, plan, *own_tables)
    v_half, part = pl.pallas_call(
        kick_kernel,
        out_shape=(force, jax.ShapeDtypeStruct((8, CELL), F32)),
        in_specs=[VMEM] * 7,
        out_specs=(VMEM, VMEM),
        compiler_params=limit(2),
        name="kick",
    )(own, other, short_own, short_a, short_b, par, speed)
    if slabs <= 4:
        parts = [part]
        for step in range(1, slabs):
            route = [(i, (i + step) % slabs) for i in range(slabs)]
            parts.append(lax.ppermute(part, "brick", route))
    else:
        parts = [lax.psum(part, "brick")]
    moved = jax.ShapeDtypeStruct((3, 1, count), F32)
    new_positions, new_velocities = pl.pallas_call(
        functools.partial(drift_kernel, freedom=3 * count * slabs),
        out_shape=(moved, moved),
        in_specs=[VMEM] * (len(parts) + 2) + [SMEM],
        out_specs=(VMEM, VMEM),
        compiler_params=limit(2),
        name="drift",
    )(*parts, v_half, mine, target_warmth_levels)
    return (
        jnp.transpose(new_positions, (1, 0, 2)),
        jnp.transpose(new_velocities, (1, 0, 2)),
        deviation,
    )


def solution(mesh):
    return jax.shard_map(
        local,
        mesh=mesh,
        in_specs=(
            P("replica", None, "brick"),
            P("replica", None, "brick"),
            P("brick"),
            P("brick"),
            P("brick"),
            P("brick"),
            P("brick"),
            P("brick", None, None),
            P("brick", None, None),
            P("brick", None),
            P("brick"),
            P(None, "brick"),
            P("replica"),
        ),
        out_specs=(
            P("replica", None, "brick"),
            P("replica", None, "brick"),
            P("brick", "replica", None),
        ),
        check_vma=False,
    )
```

profile of v0, /device:TPU:0, one launch (start us, length us, event | category | flops | bytes accessed | tf_op | source)
XLA Modules:
  0.0 32.8 jit_solution(82145731127938952)
XLA Ops:
  0.6 4.1 %collective-permute-start = (f32[1,3,1,768]{3,2,1,0:T(1,128)}, f32[1,3,1,768]{3,2,1,0:T(1,128)S(1)}, u32[]{:S(2)}, u32[]{:S(2)}) collective-permute-start(f32[1,3,1,768]{3,2,1,0:T(1,128)} %bitcast.10), channel_id=1, source_target_pairs={{0,16},{4,20},{8,24},{12,28},{16,0},{20,4},{24,8},{28,12},{1,17},{... | collective-permute-start | bytes 27656 | tf_op jit(solution)/shard_map/ppermute | solution.py:537
  4.8 1.6 %prep.1 = (f32[1,3,1,768]{3,2,1,0:T(1,128)S(1)}, f32[3,1,768]{2,1,0:T(1,128)S(1)}, f32[8,768]{1,0:T(8,128)S(1)}, s32[2,8,128]{2,1,0:T(8,128)S(1)}, f32[17,16,128...) custom-call(f32[3,1,768]{2,1,0:T(1,128)} %bitcast.11, ...), custom_call_target="tpu_custom_call" | custom-call | flops 500000000 | bytes 1000000 | tf_op jit(solution)/shard_map/prep/pallas_call | solution.py:544
  6.4 0.1 collective-permute-start.5
  6.5 1.7 %collective-permute-start.6 = (f32[17,16,128]{2,1,0:T(8,128)S(1)}, f32[17,16,128]{2,1,0:T(8,128)S(1)}, u32[]{:S(2)}, u32[]{:S(2)}) collective-permute-start(f32[17,16,128]{2,1,0:T(8,128)S(1)} %get-tuple-element.53), channel_id=1, source_target_pairs={{1,0},{2,1},{3,2},{0,3},{5,4},{6,5},{7,6},{4,7},{9,8},{10,9},{11,1... | collective-permute-start | bytes 417800 | tf_op jit(solution)/shard_map/ppermute | solution.py:598
  8.2 0.0 collective-permute-done.refs_1_
  8.2 1.6 %collective-permute-start.1 = (f32[2,3,1,768]{3,2,1,0:T(1,128)S(1)}, f32[2,3,1,768]{3,2,1,0:T(1,128)S(1)}, u32[]{:S(2)}, u32[]{:S(2)}) collective-permute-start(f32[2,3,1,768]{3,2,1,0:T(1,128)S(1)} %pad_maximum_fusion.1), channel_id=1, source_target_pairs={{0,8},{4,12},{8,0},{12,4},{16,24},{20,28},{24,16},{28,20},{1,9},{5... | collective-permute-start | bytes 55304 | tf_op jit(solution)/shard_map/ppermute | solution.py:537
  9.9 1.9 %own_pairs.1 = (f32[768,128]{1,0:T(8,128)S(1)}, s32[768,128]{1,0:T(8,128)S(1)}, s32[768,128]{1,0:T(8,128)S(1)}, f32[768,128]{1,0:T(8,128)S(1)}, f32[3,512]{1,0:T(4,128)S(1)}) custom-call(f32[1,3,1,768]{3,2,1,0:T(1,128)S(1)} %get-tuple-element.40.refs_0_.mine.refs_5_, f32[8,768]{1,0:T(8,128)S(1)} %get-tuple-element.41.refs_3_.par, ...), custom_call_target="tpu_custom_call" | custom-call | flops 1000000000 | bytes 2000000 | tf_op jit(solution)/shard_map/own_pairs/pallas_call | solution.py:609
  11.8 0.3 collective-permute-done.1.refs_2_
  12.1 1.6 %collective-permute-start.2 = (f32[4,3,1,768]{3,2,1,0:T(1,128)S(1)}, f32[4,3,1,768]{3,2,1,0:T(1,128)S(1)}, u32[]{:S(2)}, u32[]{:S(2)}) collective-permute-start(f32[4,3,1,768]{3,2,1,0:T(1,128)S(1)} %pad_maximum_fusion), channel_id=1, source_target_pairs={{0,4},{4,0},{8,12},{12,8},{16,20},{20,16},{24,28},{28,24},{1,5},{5... | collective-permute-start | bytes 110600 | tf_op jit(solution)/shard_map/ppermute | solution.py:537
  13.6 1.7 %early.1.total = f32[14,64,128]{2,1,0:T(8,128)S(1)} custom-call(f32[1,3,1,768]{3,2,1,0:T(1,128)S(1)} %get-tuple-element.40.refs_0_.mine.refs_5_, f32[1,3,1,768]{3,2,1,0:T(1,128)S(1)} %collective-permute-done.refs_1_, f32[2,3,1,768]{3,2,1,0:T(1,128)S(1)} %collective-permute-done.1.refs_2_, f32[8,768]{1,0:T(8,128)S(1)} %get-tuple-element.41.refs_3_.par), custom_call_target="tpu_custom_call" | custom-call | flops 1000000000 | bytes 2000000 | tf_op jit(solution)/shard_map/early/pallas_call | solution.py:630
  15.3 0.8 %collective-permute-done.2.late = f32[4,3,1,768]{3,2,1,0:T(1,128)S(1)} collective-permute-done((f32[4,3,1,768]{3,2,1,0:T(1,128)S(1)}, f32[4,3,1,768]{3,2,1,0:T(1,128)S(1)}, u32[]{:S(2)}, u32[]{:S(2)}) %collective-permute-start.2) | collective-permute-done | bytes 36896 | tf_op jit(solution)/shard_map/ppermute | solution.py:537
  16.1 1.0 %across.1 = (f32[4,64,128]{2,1,0:T(8,128)S(1)}, bf16[6,64,128]{2,1,0:T(8,128)(2,1)S(1)}, f32[4,16,768]{2,1,0:T(8,128)S(1)}, f32[4,64,768]{2,1,0:T(8,128)S(1)}, bf16[4,128,768]{2,1,0:T(8,128)(2,1)S(1)}) custom-call(f32[4,3,1,768]{3,2,1,0:T(1,128)S(1)} %collective-permute-done.2.late, f32[8,768]{1,0:T(8,128)S(1)} %get-tuple-element.41.refs_3_.par, ...), custom_call_target="tpu_custom_call" | custom-call | flops 500000000 | bytes 1000000 | tf_op jit(solution)/shard_map/across/pallas_call | solution.py:644
  17.2 0.6 %beside.1 = (f32[4,64,128]{2,1,0:T(8,128)S(1)}, bf16[6,64,128]{2,1,0:T(8,128)(2,1)S(1)}) custom-call(f32[4,3,1,768]{3,2,1,0:T(1,128)S(1)} %collective-permute-done.2.late, f32[8,768]{1,0:T(8,128)S(1)} %get-tuple-element.41.refs_3_.par, f32[14,64,128]{2,1,0:T(8,128)S(1)} %early.1.total, f32[4,64,768]{2,1,0:T(8,128)S(1)} %get-tuple-element.44.y_in, ...), custom_call_target="tpu_custom_call" | custom-call | flops 500000000 | bytes 1000000 | tf_op jit(solution)/shard_map/beside/pallas_call | solution.py:662
  17.8 0.1 collective-permute-start.4
  17.9 1.6 %collective-permute-start.3 = (bf16[6,64,128]{2,1,0:T(8,128)(2,1)S(1)}, bf16[6,64,128]{2,1,0:T(8,128)(2,1)S(1)}, u32[]{:S(2)}, u32[]{:S(2)}) collective-permute-start(bf16[6,64,128]{2,1,0:T(8,128)(2,1)S(1)} %get-tuple-element.43), channel_id=1, source_target_pairs={{0,3},{1,2},{2,1},{3,0},{4,7},{5,6},{6,5},{7,4},{8,11},{9,10},{10,... | collective-permute-start | bytes 294920 | tf_op jit(solution)/shard_map/ppermute | solution.py:661
  19.5 0.0 collective-permute-done.5.low.near_low
  19.5 0.0 collective-permute-done.6.high.near_high
  19.5 0.3 %ghosts.1 = (f32[512,128]{1,0:T(8,128)S(1)}, s32[512,128]{1,0:T(8,128)S(1)}, s32[512,128]{1,0:T(8,128)S(1)}, f32[512,128]{1,0:T(8,128)S(1)}) custom-call(f32[17,16,128]{2,1,0:T(8,128)S(1)} %collective-permute-done.5.low.near_low, f32[17,16,128]{2,1,0:T(8,128)S(1)} %collective-permute-done.6.high.near_high), custom_call_target="tpu_custom_call" | custom-call | flops 500000000 | bytes 1000000 | tf_op jit(solution)/shard_map/ghosts/pallas_call | solution.py:619
  19.8 3.5 %middle.1 = (f32[6,64,128]{2,1,0:T(8,128)S(1)}, bf16[384,128]{1,0:T(8,128)(2,1)S(1)}, f32[3,768]{1,0:T(4,128)S(1)}, f32[3,768]{1,0:T(4,128)S(1)}) custom-call(f32[4,3,1,768]{3,2,1,0:T(1,128)S(1)} %collective-permute-done.2.late, f32[4,16,768]{2,1,0:T(8,128)S(1)} %get-tuple-element.48.x_in, f32[4,64,768]{2,1,0:T(8,128)S(1)} %get-tuple-element.44.y_in, ...), custom_call_target="tpu_custom_call" | custom-call | flops 1000000000 | bytes 2000000 | tf_op jit(solution)/shard_map/middle/pallas_call | solution.py:675
  23.3 0.0 collective-permute-done.4.got_c
  23.3 0.0 collective-permute-done.3.got_y
  23.3 0.8 %grad.1 = (f32[10,16,128]{2,1,0:T(8,128)}, bf16[896,128]{1,0:T(8,128)(2,1)S(1)}, f32[3,768]{1,0:T(4,128)S(1)}) custom-call(f32[4,3,1,768]{3,2,1,0:T(1,128)S(1)} %collective-permute-done.2.late, f32[8,768]{1,0:T(8,128)S(1)} %get-tuple-element.41.refs_3_.par, f32[4,64,128]{2,1,0:T(8,128)S(1)} %get-tuple-element.42.sent_y, ...), custom_call_target="tpu_custom_call" | custom-call | flops 500000000 | bytes 1000000 | tf_op jit(solution)/shard_map/grad/pallas_call | solution.py:690
  24.2 1.6 %collective-permute-start.7 = (f32[3,768]{1,0:T(4,128)S(1)}, f32[3,768]{1,0:T(4,128)S(1)}, u32[]{:S(2)}, u32[]{:S(2)}) collective-permute-start(f32[3,768]{1,0:T(4,128)S(1)} %get-tuple-element.67), channel_id=1, source_target_pairs={{0,4},{4,0},{8,12},{12,8},{16,20},{20,16},{24,28},{28,24},{1,5},{5... | collective-permute-start | bytes 27656 | tf_op jit(solution)/shard_map/ppermute | solution.py:712
  25.7 1.8 %force.1 = (f32[3,768]{1,0:T(4,128)S(1)}, f32[3,256]{1,0:T(4,128)S(1)}) custom-call(bf16[896,128]{1,0:T(8,128)(2,1)S(1)} %get-tuple-element.61.grad, f32[1,3,1,768]{3,2,1,0:T(1,128)S(1)} %get-tuple-element.40.refs_0_.mine.refs_5_, f32[8,768]{1,0:T(8,128)S(1)} %get-tuple-element.41.refs_3_.par, s32[2,8,128]{2,1,0:T(8,128)S(1)} %get-tuple-element.49.plan, ...), custom_call_target="tpu_custom_call" | custom-call | flops 1000000000 | bytes 2000000 | tf_op jit(solution)/shard_map/force/pallas_call | solution.py:713
  27.5 0.4 %collective-permute-done.7.other = f32[3,768]{1,0:T(4,128)S(1)} collective-permute-done((f32[3,768]{1,0:T(4,128)S(1)}, f32[3,768]{1,0:T(4,128)S(1)}, u32[]{:S(2)}, u32[]{:S(2)}) %collective-permute-start.7) | collective-permute-done | bytes 9248 | tf_op jit(solution)/shard_map/ppermute | solution.py:712
  28.0 0.1 kick.1
  28.1 0.0 collective-permute-start.10
  28.1 0.5 %collective-permute-start.8 = (f32[8,128]{1,0:T(8,128)S(1)}, f32[8,128]{1,0:T(8,128)S(1)}, u32[]{:S(2)}, u32[]{:S(2)}) collective-permute-start(f32[8,128]{1,0:T(8,128)S(1)} %get-tuple-element.72.refs_0_), channel_id=1, source_target_pairs={{0,1},{1,2},{2,3},{3,0},{4,5},{5,6},{6,7},{7,4},{8,9},{9,10},{10,1... | collective-permute-start | bytes 12296 | tf_op jit(solution)/shard_map/ppermute | solution.py:735
  28.6 0.6 %collective-permute-start.9 = (f32[8,128]{1,0:T(8,128)S(1)}, f32[8,128]{1,0:T(8,128)S(1)}, u32[]{:S(2)}, u32[]{:S(2)}) collective-permute-start(f32[8,128]{1,0:T(8,128)S(1)} %get-tuple-element.72.refs_0_), channel_id=1, source_target_pairs={{0,2},{1,3},{2,0},{3,1},{4,6},{5,7},{6,4},{7,5},{8,10},{9,11},{10,... | collective-permute-start | bytes 12296 | tf_op jit(solution)/shard_map/ppermute | solution.py:735
  29.8 0.0 collective-permute-done.10.refs_3_
  29.8 1.3 %collective-permute-done.8.refs_1_ = f32[8,128]{1,0:T(8,128)S(1)} collective-permute-done((f32[8,128]{1,0:T(8,128)S(1)}, f32[8,128]{1,0:T(8,128)S(1)}, u32[]{:S(2)}, u32[]{:S(2)}) %collective-permute-start.8) | collective-permute-done | bytes 4128 | tf_op jit(solution)/shard_map/ppermute | solution.py:735
  31.1 1.0 %collective-permute-done.9.refs_2_ = f32[8,128]{1,0:T(8,128)S(1)} collective-permute-done((f32[8,128]{1,0:T(8,128)S(1)}, f32[8,128]{1,0:T(8,128)S(1)}, u32[]{:S(2)}, u32[]{:S(2)}) %collective-permute-start.9) | collective-permute-done | bytes 4128 | tf_op jit(solution)/shard_map/ppermute | solution.py:735
  32.2 0.6 %drift.1 = (f32[3,1,768]{2,1,0:T(1,128)}, f32[3,1,768]{2,1,0:T(1,128)}) custom-call(f32[8,128]{1,0:T(8,128)S(1)} %get-tuple-element.72.refs_0_, f32[8,128]{1,0:T(8,128)S(1)} %collective-permute-done.8.refs_1_, f32[8,128]{1,0:T(8,128)S(1)} %collective-permute-done.9.refs_2_, f32[8,128]{1,0:T(8,128)S(1)} %collective-permute-done.10.refs_3_, ...), custom_call_target="tpu_custom_call" | custom-call | tf_op jit(solution)/shard_map/drift/pallas_call | solution.py:739
  (2 shorter events, 0.1 us)
Async XLA Ops:
  0.6 7.6 %collective-permute-start = (f32[1,3,1,768]{3,2,1,0:T(1,128)}, f32[1,3,1,768]{3,2,1,0:T(1,128)S(1)}, u32[]{:S(2)}, u32[]{:S(2)}) collective-permute-start(f32[1,3,1,768]{3,2,1,0:T(1,128)} %bitcast.10), channel_id=1, source_target_pairs={{0,16},{4,20},{8,24},{12,28},{16,0},{20,4},{24,8},{28,12},{1,17},{... | collective-permute-start | bytes 27656 | tf_op jit(solution)/shard_map/ppermute | solution.py:537
  6.4 13.1 %collective-permute-start.5 = (f32[17,16,128]{2,1,0:T(8,128)S(1)}, f32[17,16,128]{2,1,0:T(8,128)S(1)}, u32[]{:S(2)}, u32[]{:S(2)}) collective-permute-start(f32[17,16,128]{2,1,0:T(8,128)S(1)} %get-tuple-element.52), channel_id=1, source_target_pairs={{0,1},{1,2},{2,3},{3,0},{4,5},{5,6},{6,7},{7,4},{8,9},{9,10},{10,1... | collective-permute-start | bytes 417800 | tf_op jit(solution)/shard_map/ppermute | solution.py:597
  6.5 13.0 %collective-permute-start.6 = (f32[17,16,128]{2,1,0:T(8,128)S(1)}, f32[17,16,128]{2,1,0:T(8,128)S(1)}, u32[]{:S(2)}, u32[]{:S(2)}) collective-permute-start(f32[17,16,128]{2,1,0:T(8,128)S(1)} %get-tuple-element.53), channel_id=1, source_target_pairs={{1,0},{2,1},{3,2},{0,3},{5,4},{6,5},{7,6},{4,7},{9,8},{10,9},{11,1... | collective-permute-start | bytes 417800 | tf_op jit(solution)/shard_map/ppermute | solution.py:598
  8.2 3.8 %collective-permute-start.1 = (f32[2,3,1,768]{3,2,1,0:T(1,128)S(1)}, f32[2,3,1,768]{3,2,1,0:T(1,128)S(1)}, u32[]{:S(2)}, u32[]{:S(2)}) collective-permute-start(f32[2,3,1,768]{3,2,1,0:T(1,128)S(1)} %pad_maximum_fusion.1), channel_id=1, source_target_pairs={{0,8},{4,12},{8,0},{12,4},{16,24},{20,28},{24,16},{28,20},{1,9},{5... | collective-permute-start | bytes 55304 | tf_op jit(solution)/shard_map/ppermute | solution.py:537
  12.1 4.0 %collective-permute-start.2 = (f32[4,3,1,768]{3,2,1,0:T(1,128)S(1)}, f32[4,3,1,768]{3,2,1,0:T(1,128)S(1)}, u32[]{:S(2)}, u32[]{:S(2)}) collective-permute-start(f32[4,3,1,768]{3,2,1,0:T(1,128)S(1)} %pad_maximum_fusion), channel_id=1, source_target_pairs={{0,4},{4,0},{8,12},{12,8},{16,20},{20,16},{24,28},{28,24},{1,5},{5... | collective-permute-start | bytes 110600 | tf_op jit(solution)/shard_map/ppermute | solution.py:537
  17.8 5.5 %collective-permute-start.4 = (bf16[6,64,128]{2,1,0:T(8,128)(2,1)S(1)}, bf16[6,64,128]{2,1,0:T(8,128)(2,1)S(1)}, u32[]{:S(2)}, u32[]{:S(2)}) collective-permute-start(bf16[6,64,128]{2,1,0:T(8,128)(2,1)S(1)} %get-tuple-element.47), channel_id=1, source_target_pairs={{0,1},{1,0},{2,3},{3,2},{4,5},{5,4},{6,7},{7,6},{8,9},{9,8},{10,11... | collective-permute-start | bytes 294920 | tf_op jit(solution)/shard_map/ppermute | solution.py:672
  17.9 5.5 %collective-permute-start.3 = (bf16[6,64,128]{2,1,0:T(8,128)(2,1)S(1)}, bf16[6,64,128]{2,1,0:T(8,128)(2,1)S(1)}, u32[]{:S(2)}, u32[]{:S(2)}) collective-permute-start(bf16[6,64,128]{2,1,0:T(8,128)(2,1)S(1)} %get-tuple-element.43), channel_id=1, source_target_pairs={{0,3},{1,2},{2,1},{3,0},{4,7},{5,6},{6,5},{7,4},{8,11},{9,10},{10,... | collective-permute-start | bytes 294920 | tf_op jit(solution)/shard_map/ppermute | solution.py:661
  24.2 3.8 %collective-permute-start.7 = (f32[3,768]{1,0:T(4,128)S(1)}, f32[3,768]{1,0:T(4,128)S(1)}, u32[]{:S(2)}, u32[]{:S(2)}) collective-permute-start(f32[3,768]{1,0:T(4,128)S(1)} %get-tuple-element.67), channel_id=1, source_target_pairs={{0,4},{4,0},{8,12},{12,8},{16,20},{20,16},{24,28},{28,24},{1,5},{5... | collective-permute-start | bytes 27656 | tf_op jit(solution)/shard_map/ppermute | solution.py:712
  28.1 1.8 %collective-permute-start.10 = (f32[8,128]{1,0:T(8,128)S(1)}, f32[8,128]{1,0:T(8,128)S(1)}, u32[]{:S(2)}, u32[]{:S(2)}) collective-permute-start(f32[8,128]{1,0:T(8,128)S(1)} %get-tuple-element.72.refs_0_), channel_id=1, source_target_pairs={{0,3},{1,0},{2,1},{3,2},{4,7},{5,4},{6,5},{7,6},{8,11},{9,8},{10,9... | collective-permute-start | bytes 12296 | tf_op jit(solution)/shard_map/ppermute | solution.py:735
  28.1 3.1 %collective-permute-start.8 = (f32[8,128]{1,0:T(8,128)S(1)}, f32[8,128]{1,0:T(8,128)S(1)}, u32[]{:S(2)}, u32[]{:S(2)}) collective-permute-start(f32[8,128]{1,0:T(8,128)S(1)} %get-tuple-element.72.refs_0_), channel_id=1, source_target_pairs={{0,1},{1,2},{2,3},{3,0},{4,5},{5,6},{6,7},{7,4},{8,9},{9,10},{10,1... | collective-permute-start | bytes 12296 | tf_op jit(solution)/shard_map/ppermute | solution.py:735
  28.6 3.6 %collective-permute-start.9 = (f32[8,128]{1,0:T(8,128)S(1)}, f32[8,128]{1,0:T(8,128)S(1)}, u32[]{:S(2)}, u32[]{:S(2)}) collective-permute-start(f32[8,128]{1,0:T(8,128)S(1)} %get-tuple-element.72.refs_0_), channel_id=1, source_target_pairs={{0,2},{1,3},{2,0},{3,1},{4,6},{5,7},{6,4},{7,5},{8,10},{9,11},{10,... | collective-permute-start | bytes 12296 | tf_op jit(solution)/shard_map/ppermute | solution.py:735
where the time goes:
time: 33 us; the launch traced here: 32.8 us
  Pallas kernels  14 us (42%)
  starting transfers between devices  13.5 us (41%)
  waiting for transfers between devices  3.86 us (12%)
  between operations  1.4 us (4%)
    ppermute x3, starting transfers between devices, hop(): lax.ppermute(known, 'replica', [(i, i ^ mask) for i in range(members)])  7.33 us
    pallas_call x1, Pallas kernels, local(): pl.pallas_call(functools.partial(middle_kernel, **place, members=members)...  3.48 us
    ppermute x3, waiting for transfers between devices, local(): parts.append(lax.ppermute(part, 'brick', route))  2.36 us
    pallas_call x1, Pallas kernels, local(): pl.pallas_call(own_kernel, out_shape=(*tables(cells), jax.ShapeDtypeStruc...  1.88 us
    pallas_call x1, Pallas kernels, local(): pl.pallas_call(functools.partial(force_kernel, **place, first=now), out_s...  1.78 us
    ppermute x1, starting transfers between devices, local(): near_high = lax.ppermute(near_down, 'brick', back)  1.73 us
    pallas_call x1, Pallas kernels, local(): pl.pallas_call(functools.partial(early_kernel, **place), out_shape=jax.Sh...  1.68 us
    pallas_call x1, Pallas kernels, local(): pl.pallas_call(functools.partial(prep_kernel, thick=thick, bit=bit, half=...  1.63 us
  transfers between devices with their start and end apart: 11, of which 5 were waited for; matrix products, arithmetic and copies ran while one was open for 0% of the time, Pallas kernels for 38%

commit v1 on v0

--- a/solution.py
+++ b/solution.py
@@ -27,20 +27,32 @@
 HBM = pl.BlockSpec(memory_space=pltpu.HBM)
 
 
-def bell(grid, coord, rate, period=None):
+def fixed(v, unit):
+    whole = jnp.floor(v)
+    part = ((v - whole) * float(unit)).astype(jnp.int32)
+    return (whole.astype(jnp.int32) << (unit.bit_length() - 1)) + part
+
+
+def bell(grid, coord, rate):
     delta = grid - coord
-    if period is not None:
-        away = jnp.abs(delta)
-        delta = jnp.minimum(away, period - away)
     return jnp.exp2(delta * delta * rate)
 
 
-def bell_slope(grid, coord, inv_var, rate, period=None):
+def ring_bell(grid, coord, rate, unit):
+    delta = (grid - fixed(coord, unit)).astype(F32)
+    return jnp.exp2(delta * delta * (rate * (1.0 / unit / unit)))
+
+
+def bell_slope(grid, coord, inv_var, rate):
     delta = grid - coord
-    if period is not None:
-        delta = delta - period * jnp.floor(delta * (1.0 / period) + 0.5)
     value = jnp.exp2(delta * delta * rate)
     return value, delta * inv_var * value
+
+
+def ring_bell_slope(grid, coord, inv_var, rate, unit):
+    delta = (grid - fixed(coord, unit)).astype(F32)
+    value = jnp.exp2(delta * delta * (rate * (1.0 / unit / unit)))
+    return value, delta * (inv_var * (1.0 / unit)) * value
 
 
 def limit(mib):
@@ -70,7 +82,7 @@
 def local_rows(shape, member, bit, block):
     row = iota(shape, 0)
     own = (member >> bit) & 1
-    return ((row // block) * (2 * block) + own * block + row % block).astype(F32)
+    return (row // block) * (2 * block) + own * block + row % block
 
 
 def prep_kernel(
@@ -164,19 +176,25 @@
         copy.wait()
 
 
+def ring_unit(period):
+    unit = 2**32 // period
+    assert unit * period == 2**32
+    return unit
+
+
 def spread_grids(half, depth, count, thick, bit, block):
     first = lax.axis_index("brick") * thick - HALO
     x_grid = (iota((16, count), 0) + first).astype(F32)
-    y_grid = local_rows((half, count), lax.axis_index("replica"), bit, block)
-    z_grid = iota((depth, count), 0).astype(F32)
+    y_grid = local_rows((half, count), lax.axis_index("replica"), bit, block) * ring_unit(2 * half)
+    z_grid = iota((depth, count), 0) * ring_unit(depth)
     return x_grid, y_grid, z_grid
 
 
 def member_bells(place, amp, rate, grids):
     x_grid, y_grid, z_grid = grids
     x_amp = amp * bell(x_grid, place[0], rate)
-    y_val = bell(y_grid, place[1], rate, 2 * y_grid.shape[0])
-    z_val = bell(z_grid, place[2], rate, z_grid.shape[0]).astype(BF16)
+    y_val = ring_bell(y_grid, place[1], rate, ring_unit(2 * y_grid.shape[0]))
+    z_val = ring_bell(z_grid, place[2], rate, ring_unit(z_grid.shape[0])).astype(BF16)
     return x_amp, y_val, z_val
 
 
@@ -275,21 +293,13 @@
     pack_rim(out, packet, base)
 
 
-FIXED = float(2**25)
-
-
-def fixed(v):
-    whole = jnp.floor(v)
-    return (whole.astype(jnp.int32) << 25) + ((v - whole) * FIXED).astype(jnp.int32)
-
-
-def enter(tables, n, x, y, z, q):
+def enter(tables, n, x, y, z, q, unit):
     at = slice(n * CELL, (n + 1) * CELL)
-    for table, row in zip(tables, (x * FIXED, fixed(y), fixed(z), q)):
+    for table, row in zip(tables, (x * float(unit), fixed(y, unit), fixed(z, unit), q)):
         table[at, :] = jnp.broadcast_to(row, (CELL, CELL)).T
 
 
-def ghost_kernel(low, high, *tables, n_x, ghosts):
+def ghost_kernel(low, high, *tables, n_x, ghosts, unit):
     slabs = lax.axis_size("brick")
     brick = lax.axis_index("brick")
     last = low.shape[0] - 1
@@ -298,33 +308,35 @@
     for n, (ref, shift) in enumerate(((low, shift_low), (high, shift_high))):
         for g in range(ghosts):
             row = [ref[last, k * ghosts + g : k * ghosts + g + 1, :] for k in range(4)]
-            enter(tables, n * ghosts + g, row[0] + shift, row[1], row[2], row[3])
-
-
-def own_kernel(mine, par, plan, *refs):
+            enter(tables, n * ghosts + g, row[0] + shift, row[1], row[2], row[3], unit)
+
+
+def own_kernel(mine, par, plan, *refs, unit, cells):
     tables, (out, plan_s, sem) = refs[:4], refs[4:]
     copy = pltpu.make_async_copy(plan, plan_s, sem)
     copy.start()
     for c in range(mine.shape[3] // CELL):
         at = slice(c * CELL, (c + 1) * CELL)
-        enter(tables, c, mine[0, 0, :, at], mine[0, 1, :, at], mine[0, 2, :, at], par[1:2, at])
+        place = [mine[0, k, :, at] for k in range(3)]
+        enter(tables, c, *place, par[1:2, at], unit)
     copy.wait()
-    pair_cells(mine, par, [tables], [0], plan_s, out, 0)
+    pair_cells(mine, par, {0: tables}, plan_s, out, cells, unit)
 
 
 COUNT_AT = 127
 
 
-def pair_cells(mine, par, kinds, which, plan, out, first):
-    for c in range(first, first + out.shape[1] // CELL):
+def pair_cells(mine, par, tables, plan, out, work, unit):
+    one = float(unit)
+    for n, (c, kinds) in enumerate(work):
         at = slice(c * CELL, (c + 1) * CELL)
-        xi = jnp.broadcast_to(mine[0, 0, :, at] * FIXED, (8, CELL))
-        yi = jnp.broadcast_to(fixed(mine[0, 1, :, at]), (8, CELL))
-        zi = jnp.broadcast_to(fixed(mine[0, 2, :, at]), (8, CELL))
+        xi = jnp.broadcast_to(mine[0, 0, :, at] * one, (8, CELL))
+        yi = jnp.broadcast_to(fixed(mine[0, 1, :, at], unit), (8, CELL))
+        zi = jnp.broadcast_to(fixed(mine[0, 2, :, at], unit), (8, CELL))
         zero = jnp.zeros((8, CELL), F32)
         total = (zero, zero, zero)
-        for kind, tables in zip(which, kinds):
-            place_x, place_y, place_z, load = tables
+        for kind in kinds:
+            place_x, place_y, place_z, load = tables[kind]
 
             def slot(s, total):
                 start = pl.multiple_of(plan[kind, c, s] * CELL, CELL)
@@ -334,7 +346,7 @@
                     dx = xi - place_x[here, :]
                     dy = (yi - place_y[here, :]).astype(F32)
                     dz = (zi - place_z[here, :]).astype(F32)
-                    dist = dx * dx + dy * dy + (dz * dz + softening * FIXED * FIXED)
+                    dist = dx * dx + dy * dy + (dz * dz + softening * one * one)
                     inv = lax.rsqrt(dist)
                     w = load[here, :] * inv * (inv * inv)
                     tx, ty, tz = tx + w * dx, ty + w * dy, tz + w * dz
@@ -346,14 +358,15 @@
             slots = plan[kind, c, COUNT_AT]
             total = lax.fori_loop(0, slots // 2, two_slots, total)
             total = lax.fori_loop(2 * (slots // 2), slots, slot, total)
-        factor = (coupling * FIXED * FIXED) * par[1:2, at]
-        here = slice((c - first) * CELL, (c - first + 1) * CELL)
+        factor = (coupling * one * one) * par[1:2, at]
+        here = slice(n * CELL, (n + 1) * CELL)
         for k in range(3):
             out[k : k + 1, here] = factor * jnp.sum(total[k], axis=0, keepdims=True)
 
 
 def middle_kernel(
-    late, x_in, y_in, z_in, total, mine, par, plan, obs, weight, *refs, thick, bit, block, members
+    late, x_in, y_in, z_in, total, mine, par, plan, obs, weight, *refs,
+    thick, bit, block, members, unit, work,
 ):
     ghosts, (dev_out, grad, partner_out, short, left_a, left_b, plan_s, sem) = refs[:4], refs[4:]
     copy = pltpu.make_async_copy(plan, plan_s, sem)
@@ -369,7 +382,7 @@
         got = product(lefts[m % 2], z_in[m], dev_out.shape)
         dev_out[...] = got + (total[RIM:thick] if m == 0 else dev_out[...])
     for n, i in enumerate(planes):
-        dev = dev_out[n] / members - obs[i - HALO]
+        dev = dev_out[n] * (1.0 / members) - obs[i - HALO]
         dev_out[n] = dev
         grad[n * half : (n + 1) * half, :] = (restraint * weight[i - HALO] * dev).astype(BF16)
     member_force(
@@ -377,7 +390,7 @@
         planes=planes, half=half, thick=thick, bit=bit, block=block,
     )
     copy.wait()
-    pair_cells(mine, par, [ghosts], [1], plan_s, short, 0)
+    pair_cells(mine, par, {1: ghosts}, plan_s, short, work, unit)
 
 
 def member_force(place, par, grad, out, *, planes, half, thick, bit, block, plus=None):
@@ -388,8 +401,8 @@
         at = slice(t * CELL, (t + 1) * CELL)
         inv_var, rate = par[2:3, at], par[3:4, at]
         x_val, x_der = bell_slope(x_grid, place[0, :, at], inv_var, rate)
-        y_val, y_der = bell_slope(y_grid, place[1, :, at], inv_var, rate, 2 * half)
-        z_val, z_der = bell_slope(z_grid, place[2, :, at], inv_var, rate, depth)
+        y_val, y_der = ring_bell_slope(y_grid, place[1, :, at], inv_var, rate, ring_unit(2 * half))
+        z_val, z_der = ring_bell_slope(z_grid, place[2, :, at], inv_var, rate, ring_unit(depth))
         z_pair = jnp.concatenate([z_val, z_der], 1).astype(BF16)
         got = jnp.dot(grad[...], z_pair, preferred_element_type=F32)
         sums = [jnp.zeros((8, CELL), F32) for _ in range(3)]
@@ -437,7 +450,7 @@
             wanted, trust = near_rows(near_high, 0, beyond), near_rows(near_high, 1, beyond)
         else:
             wanted, trust = obs[i - HALO], weight[i - HALO]
-        dev = summed / members - wanted
+        dev = summed * (1.0 / members) - wanted
         slope = (restraint * trust * dev).astype(BF16)
         grad_rim[at * half : (at + 1) * half, :] = slope
         grad[i * half : (i + 1) * half, :] = slope
@@ -459,25 +472,37 @@
     )
 
 
-def force_kernel(grad, mine, par, plan, *refs, thick, bit, block, first):
-    own, (out, short, plan_s, sem) = refs[:4], refs[4:]
-    copy = pltpu.make_async_copy(plan, plan_s, sem)
-    copy.start()
+def force_kernel(
+    grad, deviation, mine, par, plan, *refs, thick, bit, block, unit, work
+):
+    own, ghosts, refs = refs[:4], refs[4:8], refs[8:]
+    dev_out, out, short, plan_s, sem, dev_sem = refs
+    copies = [
+        pltpu.make_async_copy(plan, plan_s, sem),
+        pltpu.make_async_copy(deviation, dev_out, dev_sem),
+    ]
+    for copy in copies:
+        copy.start()
     planes = range(thick + 2 * HALO)
     half = grad.shape[0] // len(planes)
     member_force(
         mine.at[0], par, grad, out, planes=planes, half=half, thick=thick, bit=bit, block=block
     )
-    copy.wait()
-    pair_cells(mine, par, [own], [0], plan_s, short, first)
-
-
-def kick_kernel(own, other, short_own, short_a, short_b, par, speed, v_half, part):
+    copies[0].wait()
+    pair_cells(mine, par, {0: own, 1: ghosts}, plan_s, short, work, unit)
+    copies[1].wait()
+
+
+def kick_kernel(own, other, short_own, short_a, short_b, par, speed, v_half, part, *, works):
     mass = par[4:5]
     energy = jnp.zeros_like(mass)
     for k in range(3):
-        short = jnp.concatenate([short_own[k : k + 1], short_b[k : k + 1]], 1)
-        short = short + short_a[k : k + 1]
+        shorts = {}
+        for short, work in zip((short_own, short_a, short_b), works):
+            for n, (c, _) in enumerate(work):
+                term = short[k : k + 1, n * CELL : (n + 1) * CELL]
+                shorts[c] = shorts[c] + term if c in shorts else term
+        short = jnp.concatenate([shorts[c] for c in sorted(shorts)], 1)
         force = own[k : k + 1] + other[k : k + 1] + short
         v = speed[k] + timestep * force / mass
         v_half[k : k + 1] = v
@@ -598,7 +623,17 @@
     near_high = lax.ppermute(near_down, "brick", back)
 
     cells = count // CELL
-    now = 2 * cells // 3
+    unit = ring_unit(rows)
+    assert rows == depth and members & (members - 1) == 0
+    first_cells = 2 * cells // 3
+    works = (
+        [(c, [0]) for c in range(first_cells)],
+        [(c, [1]) for c in range(cells - 1)],
+        [(c, [0]) for c in range(first_cells, cells - 1)] + [(cells - 1, [0, 1])],
+    )
+
+    def shorts(work):
+        return jax.ShapeDtypeStruct((3, len(work) * CELL), F32)
 
     def tables(blocks):
         table = jax.ShapeDtypeStruct((blocks * CELL, CELL), F32)
@@ -607,8 +642,8 @@
 
     planned = [pltpu.SMEM(plan.shape, jnp.int32), pltpu.SemaphoreType.DMA]
     *own_tables, short_own = pl.pallas_call(
-        own_kernel,
-        out_shape=(*tables(cells), jax.ShapeDtypeStruct((3, now * CELL), F32)),
+        functools.partial(own_kernel, unit=unit, cells=works[0]),
+        out_shape=(*tables(cells), shorts(works[0])),
         in_specs=[VMEM] * 3,
         out_specs=(VMEM,) * 5,
         scratch_shapes=planned,
@@ -617,7 +652,7 @@
         name="own_pairs",
     )(mine, par, plan)
     ghost_tables = pl.pallas_call(
-        functools.partial(ghost_kernel, n_x=n_x, ghosts=ghosts // CELL),
+        functools.partial(ghost_kernel, n_x=n_x, ghosts=ghosts // CELL, unit=unit),
         out_shape=tables(2 * ghosts // CELL),
         in_specs=[VMEM] * 2,
         out_specs=(VMEM,) * 4,
@@ -673,12 +708,12 @@
     force = jax.ShapeDtypeStruct((3, count), F32)
     inner = thick - RIM
     dev_middle, grad_middle, partner_middle, short_a = pl.pallas_call(
-        functools.partial(middle_kernel, **place, members=members),
+        functools.partial(middle_kernel, **place, members=members, unit=unit, work=works[1]),
         out_shape=(
             jax.ShapeDtypeStruct((inner, half, depth), F32),
             jax.ShapeDtypeStruct((inner * half, depth), BF16),
             force,
-            force,
+            shorts(works[1]),
         ),
         in_specs=[VMEM] * 14,
         out_specs=(VMEM,) * 4,
@@ -710,29 +745,32 @@
 
     swap = [(i, i ^ (1 << bit)) for i in range(members)]
     other = lax.ppermute(partner, "replica", swap)
-    own, short_b = pl.pallas_call(
-        functools.partial(force_kernel, **place, first=now),
-        out_shape=(force, jax.ShapeDtypeStruct((3, count - now * CELL), F32)),
-        in_specs=[VMEM] * 8,
-        out_specs=(VMEM, VMEM),
-        scratch_shapes=planned,
+    deviation, own, short_b = pl.pallas_call(
+        functools.partial(force_kernel, **place, unit=unit, work=works[2]),
+        out_shape=(
+            jax.ShapeDtypeStruct(deviation.shape, F32),
+            force,
+            shorts(works[2]),
+        ),
+        in_specs=[VMEM] * 13,
+        out_specs=(HBM, VMEM, VMEM),
+        scratch_shapes=planned + [pltpu.SemaphoreType.DMA],
         compiler_params=limit(8),
         cost_estimate=cost(2),
         name="force",
-    )(grad, mine, par, plan, *own_tables)
+    )(grad, deviation, mine, par, plan, *own_tables, *ghost_tables)
     v_half, part = pl.pallas_call(
-        kick_kernel,
+        functools.partial(kick_kernel, works=works),
         out_shape=(force, jax.ShapeDtypeStruct((8, CELL), F32)),
         in_specs=[VMEM] * 7,
         out_specs=(VMEM, VMEM),
         compiler_params=limit(2),
         name="kick",
     )(own, other, short_own, short_a, short_b, par, speed)
-    if slabs <= 4:
+    if slabs == 4:
         parts = [part]
-        for step in range(1, slabs):
-            route = [(i, (i + step) % slabs) for i in range(slabs)]
-            parts.append(lax.ppermute(part, "brick", route))
+        for mask in (2, 3, 1):
+            parts.append(lax.ppermute(part, "brick", [(i, i ^ mask) for i in range(slabs)]))
     else:
         parts = [lax.psum(part, "brick")]
     moved = jax.ShapeDtypeStruct((3, 1, count), F32)

time: 33 us -> 32.5 us (0.985)
  waiting for transfers between devices: 3.86 us -> 2.72 us
  starting transfers between devices: 13.5 us -> 14.2 us
    ppermute x3, waiting for transfers between devices: 2.36 us -> 1.44 us  [local(): lax.ppermute(part, 'brick', [(i, i ^ mask) for i in range(slabs)])]
    ppermute x3, starting transfers between devices: 1.1 us -> 1.86 us  [local(): lax.ppermute(part, 'brick', [(i, i ^ mask) for i in range(slabs)])]
where the time goes in v1:
time: 32.5 us; the launch traced here: 32.2 us
  starting transfers between devices  14.2 us (44%)
  Pallas kernels  13.9 us (43%)
  waiting for transfers between devices  2.72 us (8%)
  between operations  1.4 us (4%)
    ppermute x3, starting transfers between devices, hop(): lax.ppermute(known, 'replica', [(i, i ^ mask) for i in range(members)])  7.33 us
    pallas_call x1, Pallas kernels, local(): pl.pallas_call(functools.partial(middle_kernel, **place, members=members,...  3.21 us
    pallas_call x1, Pallas kernels, local(): pl.pallas_call(functools.partial(force_kernel, **place, unit=unit, work=w...  2.02 us
    pallas_call x1, Pallas kernels, local(): pl.pallas_call(functools.partial(own_kernel, unit=unit, cells=works[0]),...  1.88 us
    ppermute x3, starting transfers between devices, local(): lax.ppermute(part, 'brick', [(i, i ^ mask) for i in range(slabs)])  1.86 us
    ppermute x1, starting transfers between devices, local(): near_high = lax.ppermute(near_down, 'brick', back)  1.73 us
    pallas_call x1, Pallas kernels, local(): pl.pallas_call(functools.partial(early_kernel, **place), out_shape=jax.Sh...  1.66 us
    pallas_call x1, Pallas kernels, local(): pl.pallas_call(functools.partial(prep_kernel, thick=thick, bit=bit, half=...  1.63 us
  transfers between devices with their start and end apart: 11, of which 5 were waited for; matrix products, arithmetic and copies ran while one was open for 0% of the time, Pallas kernels for 38%

profile of v1, /device:TPU:0, one launch (start us, length us, event | category | flops | bytes accessed | tf_op | source)
XLA Modules:
  0.0 32.2 jit_solution(11411629737989274085)
XLA Ops:
  0.6 4.1 %collective-permute-start = (f32[1,3,1,768]{3,2,1,0:T(1,128)}, f32[1,3,1,768]{3,2,1,0:T(1,128)S(1)}, u32[]{:S(2)}, u32[]{:S(2)}) collective-permute-start(f32[1,3,1,768]{3,2,1,0:T(1,128)} %bitcast.10), channel_id=1, source_target_pairs={{0,16},{4,20},{8,24},{12,28},{16,0},{20,4},{24,8},{28,12},{1,17},{... | collective-permute-start | bytes 27656 | tf_op jit(solution)/shard_map/ppermute | solution.py:562
  4.8 1.6 %prep.1 = (f32[1,3,1,768]{3,2,1,0:T(1,128)S(1)}, f32[3,1,768]{2,1,0:T(1,128)S(1)}, f32[8,768]{1,0:T(8,128)S(1)}, s32[2,8,128]{2,1,0:T(8,128)S(1)}, f32[17,16,128...) custom-call(f32[3,1,768]{2,1,0:T(1,128)} %bitcast.11, ...), custom_call_target="tpu_custom_call" | custom-call | flops 500000000 | bytes 1000000 | tf_op jit(solution)/shard_map/prep/pallas_call | solution.py:569
  6.4 0.1 collective-permute-start.5
  6.5 1.7 %collective-permute-start.6 = (f32[17,16,128]{2,1,0:T(8,128)S(1)}, f32[17,16,128]{2,1,0:T(8,128)S(1)}, u32[]{:S(2)}, u32[]{:S(2)}) collective-permute-start(f32[17,16,128]{2,1,0:T(8,128)S(1)} %get-tuple-element.54), channel_id=1, source_target_pairs={{1,0},{2,1},{3,2},{0,3},{5,4},{6,5},{7,6},{4,7},{9,8},{10,9},{11,1... | collective-permute-start | bytes 417800 | tf_op jit(solution)/shard_map/ppermute | solution.py:623
  8.2 0.0 collective-permute-done.refs_1_
  8.2 1.6 %collective-permute-start.1 = (f32[2,3,1,768]{3,2,1,0:T(1,128)S(1)}, f32[2,3,1,768]{3,2,1,0:T(1,128)S(1)}, u32[]{:S(2)}, u32[]{:S(2)}) collective-permute-start(f32[2,3,1,768]{3,2,1,0:T(1,128)S(1)} %pad_maximum_fusion.1), channel_id=1, source_target_pairs={{0,8},{4,12},{8,0},{12,4},{16,24},{20,28},{24,16},{28,20},{1,9},{5... | collective-permute-start | bytes 55304 | tf_op jit(solution)/shard_map/ppermute | solution.py:562
  9.9 1.9 %own_pairs.1 = (f32[768,128]{1,0:T(8,128)S(1)}, s32[768,128]{1,0:T(8,128)S(1)}, s32[768,128]{1,0:T(8,128)S(1)}, f32[768,128]{1,0:T(8,128)S(1)}, f32[3,512]{1,0:T(4,128)S(1)}) custom-call(f32[1,3,1,768]{3,2,1,0:T(1,128)S(1)} %get-tuple-element.41.refs_0_.mine.refs_5_, f32[8,768]{1,0:T(8,128)S(1)} %get-tuple-element.42.refs_3_.par, ...), custom_call_target="tpu_custom_call" | custom-call | flops 1000000000 | bytes 2000000 | tf_op jit(solution)/shard_map/own_pairs/pallas_call | solution.py:644
  11.8 0.3 collective-permute-done.1.refs_2_
  12.1 1.6 %collective-permute-start.2 = (f32[4,3,1,768]{3,2,1,0:T(1,128)S(1)}, f32[4,3,1,768]{3,2,1,0:T(1,128)S(1)}, u32[]{:S(2)}, u32[]{:S(2)}) collective-permute-start(f32[4,3,1,768]{3,2,1,0:T(1,128)S(1)} %pad_maximum_fusion), channel_id=1, source_target_pairs={{0,4},{4,0},{8,12},{12,8},{16,20},{20,16},{24,28},{28,24},{1,5},{5... | collective-permute-start | bytes 110600 | tf_op jit(solution)/shard_map/ppermute | solution.py:562
  13.6 1.7 %early.1.total = f32[14,64,128]{2,1,0:T(8,128)S(1)} custom-call(f32[1,3,1,768]{3,2,1,0:T(1,128)S(1)} %get-tuple-element.41.refs_0_.mine.refs_5_, f32[1,3,1,768]{3,2,1,0:T(1,128)S(1)} %collective-permute-done.refs_1_, f32[2,3,1,768]{3,2,1,0:T(1,128)S(1)} %collective-permute-done.1.refs_2_, f32[8,768]{1,0:T(8,128)S(1)} %get-tuple-element.42.refs_3_.par), custom_call_target="tpu_custom_call" | custom-call | flops 1000000000 | bytes 2000000 | tf_op jit(solution)/shard_map/early/pallas_call | solution.py:665
  15.3 0.8 %collective-permute-done.2.late = f32[4,3,1,768]{3,2,1,0:T(1,128)S(1)} collective-permute-done((f32[4,3,1,768]{3,2,1,0:T(1,128)S(1)}, f32[4,3,1,768]{3,2,1,0:T(1,128)S(1)}, u32[]{:S(2)}, u32[]{:S(2)}) %collective-permute-start.2) | collective-permute-done | bytes 36896 | tf_op jit(solution)/shard_map/ppermute | solution.py:562
  16.1 1.0 %across.1 = (f32[4,64,128]{2,1,0:T(8,128)S(1)}, bf16[6,64,128]{2,1,0:T(8,128)(2,1)S(1)}, f32[4,16,768]{2,1,0:T(8,128)S(1)}, f32[4,64,768]{2,1,0:T(8,128)S(1)}, bf16[4,128,768]{2,1,0:T(8,128)(2,1)S(1)}) custom-call(f32[4,3,1,768]{3,2,1,0:T(1,128)S(1)} %collective-permute-done.2.late, f32[8,768]{1,0:T(8,128)S(1)} %get-tuple-element.42.refs_3_.par, ...), custom_call_target="tpu_custom_call" | custom-call | flops 500000000 | bytes 1000000 | tf_op jit(solution)/shard_map/across/pallas_call | solution.py:679
  17.1 0.6 %beside.1 = (f32[4,64,128]{2,1,0:T(8,128)S(1)}, bf16[6,64,128]{2,1,0:T(8,128)(2,1)S(1)}) custom-call(f32[4,3,1,768]{3,2,1,0:T(1,128)S(1)} %collective-permute-done.2.late, f32[8,768]{1,0:T(8,128)S(1)} %get-tuple-element.42.refs_3_.par, f32[14,64,128]{2,1,0:T(8,128)S(1)} %early.1.total, f32[4,64,768]{2,1,0:T(8,128)S(1)} %get-tuple-element.45.y_in, ...), custom_call_target="tpu_custom_call" | custom-call | flops 500000000 | bytes 1000000 | tf_op jit(solution)/shard_map/beside/pallas_call | solution.py:697
  17.7 0.1 collective-permute-start.4
  17.8 1.6 %collective-permute-start.3 = (bf16[6,64,128]{2,1,0:T(8,128)(2,1)S(1)}, bf16[6,64,128]{2,1,0:T(8,128)(2,1)S(1)}, u32[]{:S(2)}, u32[]{:S(2)}) collective-permute-start(bf16[6,64,128]{2,1,0:T(8,128)(2,1)S(1)} %get-tuple-element.44), channel_id=1, source_target_pairs={{0,3},{1,2},{2,1},{3,0},{4,7},{5,6},{6,5},{7,4},{8,11},{9,10},{10,... | collective-permute-start | bytes 294920 | tf_op jit(solution)/shard_map/ppermute | solution.py:696
  19.4 0.0 collective-permute-done.5.low.near_low
  19.4 0.0 collective-permute-done.6.high.near_high
  19.4 0.3 %ghosts.1 = (f32[512,128]{1,0:T(8,128)S(1)}, s32[512,128]{1,0:T(8,128)S(1)}, s32[512,128]{1,0:T(8,128)S(1)}, f32[512,128]{1,0:T(8,128)S(1)}) custom-call(f32[17,16,128]{2,1,0:T(8,128)S(1)} %collective-permute-done.5.low.near_low, f32[17,16,128]{2,1,0:T(8,128)S(1)} %collective-permute-done.6.high.near_high), custom_call_target="tpu_custom_call" | custom-call | flops 500000000 | bytes 1000000 | tf_op jit(solution)/shard_map/ghosts/pallas_call | solution.py:654
  19.7 3.2 %middle.1 = (f32[6,64,128]{2,1,0:T(8,128)S(1)}, bf16[384,128]{1,0:T(8,128)(2,1)S(1)}, f32[3,768]{1,0:T(4,128)S(1)}, f32[3,640]{1,0:T(4,128)S(1)}) custom-call(f32[4,3,1,768]{3,2,1,0:T(1,128)S(1)} %collective-permute-done.2.late, f32[4,16,768]{2,1,0:T(8,128)S(1)} %get-tuple-element.49.x_in, f32[4,64,768]{2,1,0:T(8,128)S(1)} %get-tuple-element.45.y_in, ...), custom_call_target="tpu_custom_call" | custom-call | flops 1000000000 | bytes 2000000 | tf_op jit(solution)/shard_map/middle/pallas_call | solution.py:710
  22.9 0.0 collective-permute-done.4.got_c
  23.0 0.0 collective-permute-done.3.got_y
  23.0 0.8 %grad.1 = (f32[10,16,128]{2,1,0:T(8,128)S(1)}, bf16[896,128]{1,0:T(8,128)(2,1)S(1)}, f32[3,768]{1,0:T(4,128)S(1)}) custom-call(f32[4,3,1,768]{3,2,1,0:T(1,128)S(1)} %collective-permute-done.2.late, f32[8,768]{1,0:T(8,128)S(1)} %get-tuple-element.42.refs_3_.par, f32[4,64,128]{2,1,0:T(8,128)S(1)} %get-tuple-element.43.sent_y, ...), custom_call_target="tpu_custom_call" | custom-call | flops 500000000 | bytes 1000000 | tf_op jit(solution)/shard_map/grad/pallas_call | solution.py:725
  23.8 1.6 %collective-permute-start.7 = (f32[3,768]{1,0:T(4,128)S(1)}, f32[3,768]{1,0:T(4,128)S(1)}, u32[]{:S(2)}, u32[]{:S(2)}) collective-permute-start(f32[3,768]{1,0:T(4,128)S(1)} %get-tuple-element.69), channel_id=1, source_target_pairs={{0,4},{4,0},{8,12},{12,8},{16,20},{20,16},{24,28},{28,24},{1,5},{5... | collective-permute-start | bytes 27656 | tf_op jit(solution)/shard_map/ppermute | solution.py:747
  25.3 2.0 %force.1 = (f32[10,16,128]{2,1,0:T(8,128)}, f32[3,768]{1,0:T(4,128)S(1)}, f32[3,256]{1,0:T(4,128)S(1)}) custom-call(bf16[896,128]{1,0:T(8,128)(2,1)S(1)} %get-tuple-element.62.grad, f32[10,16,128]{2,1,0:T(8,128)S(1)} %get-tuple-element.63.deviation, f32[1,3,1,768]{3,2,1,0:T(1,128)S(1)} %get-tuple-element.41.refs_0_.mine.refs_5_, ...), custom_call_target="tpu_custom_call" | custom-call | flops 1000000000 | bytes 2000000 | tf_op jit(solution)/shard_map/force/pallas_call | solution.py:748
  27.4 0.2 collective-permute-done.7.other
  27.5 0.1 kick.1
  27.6 0.0 collective-permute-start.10
  27.6 0.9 %collective-permute-start.8 = (f32[8,128]{1,0:T(8,128)S(1)}, f32[8,128]{1,0:T(8,128)S(1)}, u32[]{:S(2)}, u32[]{:S(2)}) collective-permute-start(f32[8,128]{1,0:T(8,128)S(1)} %get-tuple-element.74.refs_0_), channel_id=1, source_target_pairs={{0,2},{1,3},{2,0},{3,1},{4,6},{5,7},{6,4},{7,5},{8,10},{9,11},{10,... | collective-permute-start | bytes 12296 | tf_op jit(solution)/shard_map/ppermute | solution.py:773
  28.6 0.9 %collective-permute-start.9 = (f32[8,128]{1,0:T(8,128)S(1)}, f32[8,128]{1,0:T(8,128)S(1)}, u32[]{:S(2)}, u32[]{:S(2)}) collective-permute-start(f32[8,128]{1,0:T(8,128)S(1)} %get-tuple-element.74.refs_0_), channel_id=1, source_target_pairs={{0,3},{1,2},{2,1},{3,0},{4,7},{5,6},{6,5},{7,4},{8,11},{9,10},{10,... | collective-permute-start | bytes 12296 | tf_op jit(solution)/shard_map/ppermute | solution.py:773
  30.2 0.0 collective-permute-done.10.refs_3_
  30.2 1.2 %collective-permute-done.8.refs_1_ = f32[8,128]{1,0:T(8,128)S(1)} collective-permute-done((f32[8,128]{1,0:T(8,128)S(1)}, f32[8,128]{1,0:T(8,128)S(1)}, u32[]{:S(2)}, u32[]{:S(2)}) %collective-permute-start.8) | collective-permute-done | bytes 4128 | tf_op jit(solution)/shard_map/ppermute | solution.py:773
  31.3 0.3 collective-permute-done.9.refs_2_
  31.6 0.6 %drift.1 = (f32[3,1,768]{2,1,0:T(1,128)}, f32[3,1,768]{2,1,0:T(1,128)}) custom-call(f32[8,128]{1,0:T(8,128)S(1)} %get-tuple-element.74.refs_0_, f32[8,128]{1,0:T(8,128)S(1)} %collective-permute-done.8.refs_1_, f32[8,128]{1,0:T(8,128)S(1)} %collective-permute-done.9.refs_2_, f32[8,128]{1,0:T(8,128)S(1)} %collective-permute-done.10.refs_3_, ...), custom_call_target="tpu_custom_call" | custom-call | tf_op jit(solution)/shard_map/drift/pallas_call | solution.py:777
  (2 shorter events, 0.1 us)
Async XLA Ops:
  0.6 7.6 %collective-permute-start = (f32[1,3,1,768]{3,2,1,0:T(1,128)}, f32[1,3,1,768]{3,2,1,0:T(1,128)S(1)}, u32[]{:S(2)}, u32[]{:S(2)}) collective-permute-start(f32[1,3,1,768]{3,2,1,0:T(1,128)} %bitcast.10), channel_id=1, source_target_pairs={{0,16},{4,20},{8,24},{12,28},{16,0},{20,4},{24,8},{28,12},{1,17},{... | collective-permute-start | bytes 27656 | tf_op jit(solution)/shard_map/ppermute | solution.py:562
  6.4 13.0 %collective-permute-start.5 = (f32[17,16,128]{2,1,0:T(8,128)S(1)}, f32[17,16,128]{2,1,0:T(8,128)S(1)}, u32[]{:S(2)}, u32[]{:S(2)}) collective-permute-start(f32[17,16,128]{2,1,0:T(8,128)S(1)} %get-tuple-element.53), channel_id=1, source_target_pairs={{0,1},{1,2},{2,3},{3,0},{4,5},{5,6},{6,7},{7,4},{8,9},{9,10},{10,1... | collective-permute-start | bytes 417800 | tf_op jit(solution)/shard_map/ppermute | solution.py:622
  6.5 12.9 %collective-permute-start.6 = (f32[17,16,128]{2,1,0:T(8,128)S(1)}, f32[17,16,128]{2,1,0:T(8,128)S(1)}, u32[]{:S(2)}, u32[]{:S(2)}) collective-permute-start(f32[17,16,128]{2,1,0:T(8,128)S(1)} %get-tuple-element.54), channel_id=1, source_target_pairs={{1,0},{2,1},{3,2},{0,3},{5,4},{6,5},{7,6},{4,7},{9,8},{10,9},{11,1... | collective-permute-start | bytes 417800 | tf_op jit(solution)/shard_map/ppermute | solution.py:623
  8.2 3.8 %collective-permute-start.1 = (f32[2,3,1,768]{3,2,1,0:T(1,128)S(1)}, f32[2,3,1,768]{3,2,1,0:T(1,128)S(1)}, u32[]{:S(2)}, u32[]{:S(2)}) collective-permute-start(f32[2,3,1,768]{3,2,1,0:T(1,128)S(1)} %pad_maximum_fusion.1), channel_id=1, source_target_pairs={{0,8},{4,12},{8,0},{12,4},{16,24},{20,28},{24,16},{28,20},{1,9},{5... | collective-permute-start | bytes 55304 | tf_op jit(solution)/shard_map/ppermute | solution.py:562
  12.1 4.0 %collective-permute-start.2 = (f32[4,3,1,768]{3,2,1,0:T(1,128)S(1)}, f32[4,3,1,768]{3,2,1,0:T(1,128)S(1)}, u32[]{:S(2)}, u32[]{:S(2)}) collective-permute-start(f32[4,3,1,768]{3,2,1,0:T(1,128)S(1)} %pad_maximum_fusion), channel_id=1, source_target_pairs={{0,4},{4,0},{8,12},{12,8},{16,20},{20,16},{24,28},{28,24},{1,5},{5... | collective-permute-start | bytes 110600 | tf_op jit(solution)/shard_map/ppermute | solution.py:562
  17.7 5.3 %collective-permute-start.4 = (bf16[6,64,128]{2,1,0:T(8,128)(2,1)S(1)}, bf16[6,64,128]{2,1,0:T(8,128)(2,1)S(1)}, u32[]{:S(2)}, u32[]{:S(2)}) collective-permute-start(bf16[6,64,128]{2,1,0:T(8,128)(2,1)S(1)} %get-tuple-element.48), channel_id=1, source_target_pairs={{0,1},{1,0},{2,3},{3,2},{4,5},{5,4},{6,7},{7,6},{8,9},{9,8},{10,11... | collective-permute-start | bytes 294920 | tf_op jit(solution)/shard_map/ppermute | solution.py:707
  17.8 5.2 %collective-permute-start.3 = (bf16[6,64,128]{2,1,0:T(8,128)(2,1)S(1)}, bf16[6,64,128]{2,1,0:T(8,128)(2,1)S(1)}, u32[]{:S(2)}, u32[]{:S(2)}) collective-permute-start(bf16[6,64,128]{2,1,0:T(8,128)(2,1)S(1)} %get-tuple-element.44), channel_id=1, source_target_pairs={{0,3},{1,2},{2,1},{3,0},{4,7},{5,6},{6,5},{7,4},{8,11},{9,10},{10,... | collective-permute-start | bytes 294920 | tf_op jit(solution)/shard_map/ppermute | solution.py:696
  23.8 3.8 %collective-permute-start.7 = (f32[3,768]{1,0:T(4,128)S(1)}, f32[3,768]{1,0:T(4,128)S(1)}, u32[]{:S(2)}, u32[]{:S(2)}) collective-permute-start(f32[3,768]{1,0:T(4,128)S(1)} %get-tuple-element.69), channel_id=1, source_target_pairs={{0,4},{4,0},{8,12},{12,8},{16,20},{20,16},{24,28},{28,24},{1,5},{5... | collective-permute-start | bytes 27656 | tf_op jit(solution)/shard_map/ppermute | solution.py:747
  27.6 2.5 %collective-permute-start.10 = (f32[8,128]{1,0:T(8,128)S(1)}, f32[8,128]{1,0:T(8,128)S(1)}, u32[]{:S(2)}, u32[]{:S(2)}) collective-permute-start(f32[8,128]{1,0:T(8,128)S(1)} %get-tuple-element.74.refs_0_), channel_id=1, source_target_pairs={{0,1},{1,0},{2,3},{3,2},{4,5},{5,4},{6,7},{7,6},{8,9},{9,8},{10,11... | collective-permute-start | bytes 12296 | tf_op jit(solution)/shard_map/ppermute | solution.py:773
  27.6 3.7 %collective-permute-start.8 = (f32[8,128]{1,0:T(8,128)S(1)}, f32[8,128]{1,0:T(8,128)S(1)}, u32[]{:S(2)}, u32[]{:S(2)}) collective-permute-start(f32[8,128]{1,0:T(8,128)S(1)} %get-tuple-element.74.refs_0_), channel_id=1, source_target_pairs={{0,2},{1,3},{2,0},{3,1},{4,6},{5,7},{6,4},{7,5},{8,10},{9,11},{10,... | collective-permute-start | bytes 12296 | tf_op jit(solution)/shard_map/ppermute | solution.py:773
  28.6 3.0 %collective-permute-start.9 = (f32[8,128]{1,0:T(8,128)S(1)}, f32[8,128]{1,0:T(8,128)S(1)}, u32[]{:S(2)}, u32[]{:S(2)}) collective-permute-start(f32[8,128]{1,0:T(8,128)S(1)} %get-tuple-element.74.refs_0_), channel_id=1, source_target_pairs={{0,3},{1,2},{2,1},{3,0},{4,7},{5,6},{6,5},{7,4},{8,11},{9,10},{10,... | collective-permute-start | bytes 12296 | tf_op jit(solution)/shard_map/ppermute | solution.py:773

commit v2 on v1

--- a/solution.py
+++ b/solution.py
@@ -235,18 +235,6 @@
     return thick * (odd if across else 1 - odd)
 
 
-def pack_rim(rim, packet, base):
-    packet[:RIM] = rim[...].astype(BF16)
-    exact = rim[pl.ds(jnp.where(base == 0, 0, HALO), HALO)]
-    packet[RIM:] = (exact - exact.astype(BF16).astype(F32)).astype(BF16)
-
-
-def unpack_rim(packet, n, low):
-    value = packet[n].astype(F32)
-    extra = n - HALO if low else n
-    return value + packet[RIM + extra].astype(F32) if 0 <= extra < HALO else value
-
-
 def rim_bells(base, place, amp, rate, thick):
     first = lax.axis_index("brick") * thick - HALO + base
     grid = (iota((8, amp.shape[1]), 0) + first).astype(F32)
@@ -272,7 +260,7 @@
             build(m + 1)
         got = product(lefts[m % 2], z_out[m], out.shape)
         out[...] = got + (total[pl.ds(base, RIM)] if m == 0 else out[...])
-    pack_rim(out, packet, base)
+    packet[...] = out[...].astype(BF16)
 
 
 def beside_kernel(late, par, total, y_in, z_in, out, packet, left_a, left_b, *, thick):
@@ -290,7 +278,7 @@
             build(m + 1)
         got = product(lefts[m % 2], z_in[m], out.shape)
         out[...] = got + (total[pl.ds(base, RIM)] if m == 0 else out[...])
-    pack_rim(out, packet, base)
+    packet[...] = out[...].astype(BF16)
 
 
 def enter(tables, n, x, y, z, q, unit):
@@ -440,8 +428,8 @@
     rims = [*range(RIM), *range(thick, thick + RIM)]
     for at, i in enumerate(rims):
         low, n = i < RIM, at % RIM
-        across = sent_y[n] + unpack_rim(got_y, n, low)
-        beside = sent_c[n] + unpack_rim(got_c, n, low)
+        across = sent_y[n] + got_y[n].astype(F32)
+        beside = sent_c[n] + got_c[n].astype(F32)
         summed = jnp.where(even == low, across, beside)
         if i < HALO:
             wanted, trust = near_rows(near_low, 0, i), near_rows(near_low, 1, i)
@@ -493,12 +481,13 @@
     copies[1].wait()
 
 
-def kick_kernel(own, other, short_own, short_a, short_b, par, speed, v_half, part, *, works):
+def kick_kernel(own, other, *refs, works):
+    given, (par, speed, v_half, part) = refs[:-4], refs[-4:]
     mass = par[4:5]
     energy = jnp.zeros_like(mass)
     for k in range(3):
         shorts = {}
-        for short, work in zip((short_own, short_a, short_b), works):
+        for short, work in zip(given, works):
             for n, (c, _) in enumerate(work):
                 term = short[k : k + 1, n * CELL : (n + 1) * CELL]
                 shorts[c] = shorts[c] + term if c in shorts else term
@@ -628,8 +617,8 @@
     first_cells = 2 * cells // 3
     works = (
         [(c, [0]) for c in range(first_cells)],
-        [(c, [1]) for c in range(cells - 1)],
-        [(c, [0]) for c in range(first_cells, cells - 1)] + [(cells - 1, [0, 1])],
+        [(c, [1]) for c in range(first_cells)],
+        [(c, [0, 1]) for c in range(first_cells, cells)],
     )
 
     def shorts(work):
@@ -675,7 +664,7 @@
     )(*groups, par)
     held = late.shape[0]
     rim = jax.ShapeDtypeStruct((RIM, half, depth), F32)
-    packet = jax.ShapeDtypeStruct((RIM + HALO, half, depth), BF16)
+    packet = jax.ShapeDtypeStruct((RIM, half, depth), BF16)
     sent_y, packet_y, x_late, y_late, z_late = pl.pallas_call(
         functools.partial(across_kernel, **place),
         out_shape=(

time: 32.5 us -> 32 us (0.985)
  waiting for transfers between devices: 2.72 us -> 2.33 us
  transfers between devices with their start and end apart: 11 -> 11, of which waited for: 5 -> 4; matrix products, arithmetic and copies ran while one was open for 0% -> 0% of each run, Pallas kernels for 38% -> 39%
where the time goes in v2:
time: 32 us; the launch traced here: 31.8 us
  starting transfers between devices  14.2 us (44%)
  Pallas kernels  13.8 us (43%)
  waiting for transfers between devices  2.33 us (7%)
  between operations  1.41 us (4%)
    ppermute x3, starting transfers between devices, hop(): lax.ppermute(known, 'replica', [(i, i ^ mask) for i in range(members)])  7.33 us
    pallas_call x1, Pallas kernels, local(): pl.pallas_call(functools.partial(middle_kernel, **place, members=members,...  3.09 us
    pallas_call x1, Pallas kernels, local(): pl.pallas_call(functools.partial(force_kernel, **place, unit=unit, work=w...  2.14 us
    pallas_call x1, Pallas kernels, local(): pl.pallas_call(functools.partial(own_kernel, unit=unit, cells=works[0]),...  1.88 us
    ppermute x3, starting transfers between devices, local(): lax.ppermute(part, 'brick', [(i, i ^ mask) for i in range(slabs)])  1.86 us
    ppermute x1, starting transfers between devices, local(): near_high = lax.ppermute(near_down, 'brick', back)  1.73 us
    pallas_call x1, Pallas kernels, local(): pl.pallas_call(functools.partial(early_kernel, **place), out_shape=jax.Sh...  1.66 us
    ppermute x1, starting transfers between devices, local(): got_y = lax.ppermute(packet_y, 'brick', route)  1.64 us
  transfers between devices with their start and end apart: 11, of which 4 were waited for; matrix products, arithmetic and copies ran while one was open for 0% of the time, Pallas kernels for 39%

profile of v2, /device:TPU:0, one launch (start us, length us, event | category | flops | bytes accessed | tf_op | source)
XLA Modules:
  0.0 31.8 jit_solution(17809558620331983865)
XLA Ops:
  0.6 4.1 %collective-permute-start = (f32[1,3,1,768]{3,2,1,0:T(1,128)}, f32[1,3,1,768]{3,2,1,0:T(1,128)S(1)}, u32[]{:S(2)}, u32[]{:S(2)}) collective-permute-start(f32[1,3,1,768]{3,2,1,0:T(1,128)} %bitcast.10), channel_id=1, source_target_pairs={{0,16},{4,20},{8,24},{12,28},{16,0},{20,4},{24,8},{28,12},{1,17},{... | collective-permute-start | bytes 27656 | tf_op jit(solution)/shard_map/ppermute | solution.py:551
  4.8 1.6 %prep.1 = (f32[1,3,1,768]{3,2,1,0:T(1,128)S(1)}, f32[3,1,768]{2,1,0:T(1,128)S(1)}, f32[8,768]{1,0:T(8,128)S(1)}, s32[2,8,128]{2,1,0:T(8,128)S(1)}, f32[17,16,128...) custom-call(f32[3,1,768]{2,1,0:T(1,128)} %bitcast.11, ...), custom_call_target="tpu_custom_call" | custom-call | flops 500000000 | bytes 1000000 | tf_op jit(solution)/shard_map/prep/pallas_call | solution.py:558
  6.4 0.1 collective-permute-start.5
  6.5 1.7 %collective-permute-start.6 = (f32[17,16,128]{2,1,0:T(8,128)S(1)}, f32[17,16,128]{2,1,0:T(8,128)S(1)}, u32[]{:S(2)}, u32[]{:S(2)}) collective-permute-start(f32[17,16,128]{2,1,0:T(8,128)S(1)} %get-tuple-element.54), channel_id=1, source_target_pairs={{1,0},{2,1},{3,2},{0,3},{5,4},{6,5},{7,6},{4,7},{9,8},{10,9},{11,1... | collective-permute-start | bytes 417800 | tf_op jit(solution)/shard_map/ppermute | solution.py:612
  8.2 0.0 collective-permute-done.refs_1_
  8.2 1.6 %collective-permute-start.1 = (f32[2,3,1,768]{3,2,1,0:T(1,128)S(1)}, f32[2,3,1,768]{3,2,1,0:T(1,128)S(1)}, u32[]{:S(2)}, u32[]{:S(2)}) collective-permute-start(f32[2,3,1,768]{3,2,1,0:T(1,128)S(1)} %pad_maximum_fusion.1), channel_id=1, source_target_pairs={{0,8},{4,12},{8,0},{12,4},{16,24},{20,28},{24,16},{28,20},{1,9},{5... | collective-permute-start | bytes 55304 | tf_op jit(solution)/shard_map/ppermute | solution.py:551
  9.9 1.9 %own_pairs.1 = (f32[768,128]{1,0:T(8,128)S(1)}, s32[768,128]{1,0:T(8,128)S(1)}, s32[768,128]{1,0:T(8,128)S(1)}, f32[768,128]{1,0:T(8,128)S(1)}, f32[3,512]{1,0:T(4,128)S(1)}) custom-call(f32[1,3,1,768]{3,2,1,0:T(1,128)S(1)} %get-tuple-element.41.refs_0_.mine.refs_5_, f32[8,768]{1,0:T(8,128)S(1)} %get-tuple-element.42.refs_3_.par, ...), custom_call_target="tpu_custom_call" | custom-call | flops 1000000000 | bytes 2000000 | tf_op jit(solution)/shard_map/own_pairs/pallas_call | solution.py:633
  11.8 0.3 collective-permute-done.1.refs_2_
  12.1 1.6 %collective-permute-start.2 = (f32[4,3,1,768]{3,2,1,0:T(1,128)S(1)}, f32[4,3,1,768]{3,2,1,0:T(1,128)S(1)}, u32[]{:S(2)}, u32[]{:S(2)}) collective-permute-start(f32[4,3,1,768]{3,2,1,0:T(1,128)S(1)} %pad_maximum_fusion), channel_id=1, source_target_pairs={{0,4},{4,0},{8,12},{12,8},{16,20},{20,16},{24,28},{28,24},{1,5},{5... | collective-permute-start | bytes 110600 | tf_op jit(solution)/shard_map/ppermute | solution.py:551
  13.6 1.7 %early.1.total = f32[14,64,128]{2,1,0:T(8,128)S(1)} custom-call(f32[1,3,1,768]{3,2,1,0:T(1,128)S(1)} %get-tuple-element.41.refs_0_.mine.refs_5_, f32[1,3,1,768]{3,2,1,0:T(1,128)S(1)} %collective-permute-done.refs_1_, f32[2,3,1,768]{3,2,1,0:T(1,128)S(1)} %collective-permute-done.1.refs_2_, f32[8,768]{1,0:T(8,128)S(1)} %get-tuple-element.42.refs_3_.par), custom_call_target="tpu_custom_call" | custom-call | flops 1000000000 | bytes 2000000 | tf_op jit(solution)/shard_map/early/pallas_call | solution.py:654
  15.3 0.8 %collective-permute-done.2.late = f32[4,3,1,768]{3,2,1,0:T(1,128)S(1)} collective-permute-done((f32[4,3,1,768]{3,2,1,0:T(1,128)S(1)}, f32[4,3,1,768]{3,2,1,0:T(1,128)S(1)}, u32[]{:S(2)}, u32[]{:S(2)}) %collective-permute-start.2) | collective-permute-done | bytes 36896 | tf_op jit(solution)/shard_map/ppermute | solution.py:551
  16.1 0.9 %across.1 = (f32[4,64,128]{2,1,0:T(8,128)S(1)}, bf16[4,64,128]{2,1,0:T(8,128)(2,1)S(1)}, f32[4,16,768]{2,1,0:T(8,128)S(1)}, f32[4,64,768]{2,1,0:T(8,128)S(1)}, bf16[4,128,768]{2,1,0:T(8,128)(2,1)S(1)}) custom-call(f32[4,3,1,768]{3,2,1,0:T(1,128)S(1)} %collective-permute-done.2.late, f32[8,768]{1,0:T(8,128)S(1)} %get-tuple-element.42.refs_3_.par, ...), custom_call_target="tpu_custom_call" | custom-call | flops 500000000 | bytes 1000000 | tf_op jit(solution)/shard_map/across/pallas_call | solution.py:668
  17.1 0.6 %beside.1 = (f32[4,64,128]{2,1,0:T(8,128)S(1)}, bf16[4,64,128]{2,1,0:T(8,128)(2,1)S(1)}) custom-call(f32[4,3,1,768]{3,2,1,0:T(1,128)S(1)} %collective-permute-done.2.late, f32[8,768]{1,0:T(8,128)S(1)} %get-tuple-element.42.refs_3_.par, f32[14,64,128]{2,1,0:T(8,128)S(1)} %early.1.total, f32[4,64,768]{2,1,0:T(8,128)S(1)} %get-tuple-element.45.y_in, ...), custom_call_target="tpu_custom_call" | custom-call | flops 500000000 | bytes 1000000 | tf_op jit(solution)/shard_map/beside/pallas_call | solution.py:686
  17.7 0.1 collective-permute-start.4
  17.7 1.6 %collective-permute-start.3 = (bf16[4,64,128]{2,1,0:T(8,128)(2,1)S(1)}, bf16[4,64,128]{2,1,0:T(8,128)(2,1)S(1)}, u32[]{:S(2)}, u32[]{:S(2)}) collective-permute-start(bf16[4,64,128]{2,1,0:T(8,128)(2,1)S(1)} %get-tuple-element.44), channel_id=1, source_target_pairs={{0,3},{1,2},{2,1},{3,0},{4,7},{5,6},{6,5},{7,4},{8,11},{9,10},{10,... | collective-permute-start | bytes 196616 | tf_op jit(solution)/shard_map/ppermute | solution.py:685
  19.4 0.0 collective-permute-done.5.low.near_low
  19.4 0.0 collective-permute-done.6.high.near_high
  19.4 0.3 %ghosts.1 = (f32[512,128]{1,0:T(8,128)S(1)}, s32[512,128]{1,0:T(8,128)S(1)}, s32[512,128]{1,0:T(8,128)S(1)}, f32[512,128]{1,0:T(8,128)S(1)}) custom-call(f32[17,16,128]{2,1,0:T(8,128)S(1)} %collective-permute-done.5.low.near_low, f32[17,16,128]{2,1,0:T(8,128)S(1)} %collective-permute-done.6.high.near_high), custom_call_target="tpu_custom_call" | custom-call | flops 500000000 | bytes 1000000 | tf_op jit(solution)/shard_map/ghosts/pallas_call | solution.py:643
  19.7 3.1 %middle.1 = (f32[6,64,128]{2,1,0:T(8,128)S(1)}, bf16[384,128]{1,0:T(8,128)(2,1)S(1)}, f32[3,768]{1,0:T(4,128)S(1)}, f32[3,512]{1,0:T(4,128)S(1)}) custom-call(f32[4,3,1,768]{3,2,1,0:T(1,128)S(1)} %collective-permute-done.2.late, f32[4,16,768]{2,1,0:T(8,128)S(1)} %get-tuple-element.49.x_in, f32[4,64,768]{2,1,0:T(8,128)S(1)} %get-tuple-element.45.y_in, ...), custom_call_target="tpu_custom_call" | custom-call | flops 1000000000 | bytes 2000000 | tf_op jit(solution)/shard_map/middle/pallas_call | solution.py:699
  22.8 0.0 collective-permute-done.4.got_c
  22.8 0.0 collective-permute-done.3.got_y
  22.8 0.8 %grad.1 = (f32[10,16,128]{2,1,0:T(8,128)S(1)}, bf16[896,128]{1,0:T(8,128)(2,1)S(1)}, f32[3,768]{1,0:T(4,128)S(1)}) custom-call(f32[4,3,1,768]{3,2,1,0:T(1,128)S(1)} %collective-permute-done.2.late, f32[8,768]{1,0:T(8,128)S(1)} %get-tuple-element.42.refs_3_.par, f32[4,64,128]{2,1,0:T(8,128)S(1)} %get-tuple-element.43.sent_y, ...), custom_call_target="tpu_custom_call" | custom-call | flops 500000000 | bytes 1000000 | tf_op jit(solution)/shard_map/grad/pallas_call | solution.py:714
  23.6 1.6 %collective-permute-start.7 = (f32[3,768]{1,0:T(4,128)S(1)}, f32[3,768]{1,0:T(4,128)S(1)}, u32[]{:S(2)}, u32[]{:S(2)}) collective-permute-start(f32[3,768]{1,0:T(4,128)S(1)} %get-tuple-element.69), channel_id=1, source_target_pairs={{0,4},{4,0},{8,12},{12,8},{16,20},{20,16},{24,28},{28,24},{1,5},{5... | collective-permute-start | bytes 27656 | tf_op jit(solution)/shard_map/ppermute | solution.py:736
  25.2 2.1 %force.1 = (f32[10,16,128]{2,1,0:T(8,128)}, f32[3,768]{1,0:T(4,128)S(1)}, f32[3,256]{1,0:T(4,128)S(1)}) custom-call(bf16[896,128]{1,0:T(8,128)(2,1)S(1)} %get-tuple-element.62.grad, f32[10,16,128]{2,1,0:T(8,128)S(1)} %get-tuple-element.63.deviation, f32[1,3,1,768]{3,2,1,0:T(1,128)S(1)} %get-tuple-element.41.refs_0_.mine.refs_5_, ...), custom_call_target="tpu_custom_call" | custom-call | flops 1000000000 | bytes 2000000 | tf_op jit(solution)/shard_map/force/pallas_call | solution.py:737
  27.3 0.1 collective-permute-done.7.other
  27.4 0.1 kick.1
  27.5 0.0 collective-permute-start.10
  27.5 0.3 %collective-permute-start.8 = (f32[8,128]{1,0:T(8,128)S(1)}, f32[8,128]{1,0:T(8,128)S(1)}, u32[]{:S(2)}, u32[]{:S(2)}) collective-permute-start(f32[8,128]{1,0:T(8,128)S(1)} %get-tuple-element.74.refs_0_), channel_id=1, source_target_pairs={{0,2},{1,3},{2,0},{3,1},{4,6},{5,7},{6,4},{7,5},{8,10},{9,11},{10,... | collective-permute-start | bytes 12296 | tf_op jit(solution)/shard_map/ppermute | solution.py:762
  27.8 1.5 %collective-permute-start.9 = (f32[8,128]{1,0:T(8,128)S(1)}, f32[8,128]{1,0:T(8,128)S(1)}, u32[]{:S(2)}, u32[]{:S(2)}) collective-permute-start(f32[8,128]{1,0:T(8,128)S(1)} %get-tuple-element.74.refs_0_), channel_id=1, source_target_pairs={{0,3},{1,2},{2,1},{3,0},{4,7},{5,6},{6,5},{7,4},{8,11},{9,10},{10,... | collective-permute-start | bytes 12296 | tf_op jit(solution)/shard_map/ppermute | solution.py:762
  30.0 0.0 collective-permute-done.10.refs_3_
  30.0 1.2 %collective-permute-done.8.refs_1_ = f32[8,128]{1,0:T(8,128)S(1)} collective-permute-done((f32[8,128]{1,0:T(8,128)S(1)}, f32[8,128]{1,0:T(8,128)S(1)}, u32[]{:S(2)}, u32[]{:S(2)}) %collective-permute-start.8) | collective-permute-done | bytes 4128 | tf_op jit(solution)/shard_map/ppermute | solution.py:762
  31.2 0.0 collective-permute-done.9.refs_2_
  31.2 0.6 %drift.1 = (f32[3,1,768]{2,1,0:T(1,128)}, f32[3,1,768]{2,1,0:T(1,128)}) custom-call(f32[8,128]{1,0:T(8,128)S(1)} %get-tuple-element.74.refs_0_, f32[8,128]{1,0:T(8,128)S(1)} %collective-permute-done.8.refs_1_, f32[8,128]{1,0:T(8,128)S(1)} %collective-permute-done.9.refs_2_, f32[8,128]{1,0:T(8,128)S(1)} %collective-permute-done.10.refs_3_, ...), custom_call_target="tpu_custom_call" | custom-call | tf_op jit(solution)/shard_map/drift/pallas_call | solution.py:766
  (2 shorter events, 0.1 us)
Async XLA Ops:
  0.6 7.6 %collective-permute-start = (f32[1,3,1,768]{3,2,1,0:T(1,128)}, f32[1,3,1,768]{3,2,1,0:T(1,128)S(1)}, u32[]{:S(2)}, u32[]{:S(2)}) collective-permute-start(f32[1,3,1,768]{3,2,1,0:T(1,128)} %bitcast.10), channel_id=1, source_target_pairs={{0,16},{4,20},{8,24},{12,28},{16,0},{20,4},{24,8},{28,12},{1,17},{... | collective-permute-start | bytes 27656 | tf_op jit(solution)/shard_map/ppermute | solution.py:551
  6.4 13.0 %collective-permute-start.5 = (f32[17,16,128]{2,1,0:T(8,128)S(1)}, f32[17,16,128]{2,1,0:T(8,128)S(1)}, u32[]{:S(2)}, u32[]{:S(2)}) collective-permute-start(f32[17,16,128]{2,1,0:T(8,128)S(1)} %get-tuple-element.53), channel_id=1, source_target_pairs={{0,1},{1,2},{2,3},{3,0},{4,5},{5,6},{6,7},{7,4},{8,9},{9,10},{10,1... | collective-permute-start | bytes 417800 | tf_op jit(solution)/shard_map/ppermute | solution.py:611
  6.5 12.9 %collective-permute-start.6 = (f32[17,16,128]{2,1,0:T(8,128)S(1)}, f32[17,16,128]{2,1,0:T(8,128)S(1)}, u32[]{:S(2)}, u32[]{:S(2)}) collective-permute-start(f32[17,16,128]{2,1,0:T(8,128)S(1)} %get-tuple-element.54), channel_id=1, source_target_pairs={{1,0},{2,1},{3,2},{0,3},{5,4},{6,5},{7,6},{4,7},{9,8},{10,9},{11,1... | collective-permute-start | bytes 417800 | tf_op jit(solution)/shard_map/ppermute | solution.py:612
  8.2 3.8 %collective-permute-start.1 = (f32[2,3,1,768]{3,2,1,0:T(1,128)S(1)}, f32[2,3,1,768]{3,2,1,0:T(1,128)S(1)}, u32[]{:S(2)}, u32[]{:S(2)}) collective-permute-start(f32[2,3,1,768]{3,2,1,0:T(1,128)S(1)} %pad_maximum_fusion.1), channel_id=1, source_target_pairs={{0,8},{4,12},{8,0},{12,4},{16,24},{20,28},{24,16},{28,20},{1,9},{5... | collective-permute-start | bytes 55304 | tf_op jit(solution)/shard_map/ppermute | solution.py:551
  12.1 4.0 %collective-permute-start.2 = (f32[4,3,1,768]{3,2,1,0:T(1,128)S(1)}, f32[4,3,1,768]{3,2,1,0:T(1,128)S(1)}, u32[]{:S(2)}, u32[]{:S(2)}) collective-permute-start(f32[4,3,1,768]{3,2,1,0:T(1,128)S(1)} %pad_maximum_fusion), channel_id=1, source_target_pairs={{0,4},{4,0},{8,12},{12,8},{16,20},{20,16},{24,28},{28,24},{1,5},{5... | collective-permute-start | bytes 110600 | tf_op jit(solution)/shard_map/ppermute | solution.py:551
  17.7 5.2 %collective-permute-start.4 = (bf16[4,64,128]{2,1,0:T(8,128)(2,1)S(1)}, bf16[4,64,128]{2,1,0:T(8,128)(2,1)S(1)}, u32[]{:S(2)}, u32[]{:S(2)}) collective-permute-start(bf16[4,64,128]{2,1,0:T(8,128)(2,1)S(1)} %get-tuple-element.48), channel_id=1, source_target_pairs={{0,1},{1,0},{2,3},{3,2},{4,5},{5,4},{6,7},{7,6},{8,9},{9,8},{10,11... | collective-permute-start | bytes 196616 | tf_op jit(solution)/shard_map/ppermute | solution.py:696
  17.7 5.1 %collective-permute-start.3 = (bf16[4,64,128]{2,1,0:T(8,128)(2,1)S(1)}, bf16[4,64,128]{2,1,0:T(8,128)(2,1)S(1)}, u32[]{:S(2)}, u32[]{:S(2)}) collective-permute-start(bf16[4,64,128]{2,1,0:T(8,128)(2,1)S(1)} %get-tuple-element.44), channel_id=1, source_target_pairs={{0,3},{1,2},{2,1},{3,0},{4,7},{5,6},{6,5},{7,4},{8,11},{9,10},{10,... | collective-permute-start | bytes 196616 | tf_op jit(solution)/shard_map/ppermute | solution.py:685
  23.6 3.8 %collective-permute-start.7 = (f32[3,768]{1,0:T(4,128)S(1)}, f32[3,768]{1,0:T(4,128)S(1)}, u32[]{:S(2)}, u32[]{:S(2)}) collective-permute-start(f32[3,768]{1,0:T(4,128)S(1)} %get-tuple-element.69), channel_id=1, source_target_pairs={{0,4},{4,0},{8,12},{12,8},{16,20},{20,16},{24,28},{28,24},{1,5},{5... | collective-permute-start | bytes 27656 | tf_op jit(solution)/shard_map/ppermute | solution.py:736
  27.5 2.5 %collective-permute-start.10 = (f32[8,128]{1,0:T(8,128)S(1)}, f32[8,128]{1,0:T(8,128)S(1)}, u32[]{:S(2)}, u32[]{:S(2)}) collective-permute-start(f32[8,128]{1,0:T(8,128)S(1)} %get-tuple-element.74.refs_0_), channel_id=1, source_target_pairs={{0,1},{1,0},{2,3},{3,2},{4,5},{5,4},{6,7},{7,6},{8,9},{9,8},{10,11... | collective-permute-start | bytes 12296 | tf_op jit(solution)/shard_map/ppermute | solution.py:762
  27.5 3.7 %collective-permute-start.8 = (f32[8,128]{1,0:T(8,128)S(1)}, f32[8,128]{1,0:T(8,128)S(1)}, u32[]{:S(2)}, u32[]{:S(2)}) collective-permute-start(f32[8,128]{1,0:T(8,128)S(1)} %get-tuple-element.74.refs_0_), channel_id=1, source_target_pairs={{0,2},{1,3},{2,0},{3,1},{4,6},{5,7},{6,4},{7,5},{8,10},{9,11},{10,... | collective-permute-start | bytes 12296 | tf_op jit(solution)/shard_map/ppermute | solution.py:762
  27.8 3.3 %collective-permute-start.9 = (f32[8,128]{1,0:T(8,128)S(1)}, f32[8,128]{1,0:T(8,128)S(1)}, u32[]{:S(2)}, u32[]{:S(2)}) collective-permute-start(f32[8,128]{1,0:T(8,128)S(1)} %get-tuple-element.74.refs_0_), channel_id=1, source_target_pairs={{0,3},{1,2},{2,1},{3,0},{4,7},{5,6},{6,5},{7,4},{8,11},{9,10},{10,... | collective-permute-start | bytes 12296 | tf_op jit(solution)/shard_map/ppermute | solution.py:762

commit v3 on v2

--- a/solution.py
+++ b/solution.py
@@ -208,8 +208,12 @@
     return lax.dot_general(left[...], z_val, NT, preferred_element_type=F32).reshape(shape)
 
 
-def early_kernel(*refs, thick, bit, block):
-    groups, par, out, lefts, deeps = refs[:-6], refs[-6], refs[-5], refs[-4:-2], refs[-2:]
+def early_kernel(*refs, thick, bit, block, unit, work):
+    groups, refs = refs[:-14], refs[-14:]
+    par, plan, tables, refs = refs[0], refs[1], refs[2:6], refs[6:]
+    out, short, lefts, deeps, (plan_s, sem) = refs[0], refs[1], refs[2:4], refs[4:6], refs[6:]
+    copy = pltpu.make_async_copy(plan, plan_s, sem)
+    copy.start()
     planes, half, depth = out.shape
     count = par.shape[1]
     amp, rate = par[0:1], par[3:4]
@@ -228,6 +232,8 @@
             build(m + 1)
         got = product(lefts[m % 2], deeps[m % 2][...], out.shape)
         out[...] = got if m == 0 else out[...] + got
+    copy.wait()
+    pair_cells(groups[0], par, {0: tables}, plan_s, short, work, unit)
 
 
 def rim_side(across, thick):
@@ -618,7 +624,8 @@
     works = (
         [(c, [0]) for c in range(first_cells)],
         [(c, [1]) for c in range(first_cells)],
-        [(c, [0, 1]) for c in range(first_cells, cells)],
+        [(c, [0, 1] if c > first_cells else [1]) for c in range(first_cells, cells)],
+        [(first_cells, [0])],
     )
 
     def shorts(work):
@@ -651,17 +658,18 @@
     )(near_low, near_high)
 
     place = dict(thick=thick, bit=bit, block=block)
-    total = pl.pallas_call(
-        functools.partial(early_kernel, **place),
-        out_shape=jax.ShapeDtypeStruct((planes, half, depth), F32),
-        in_specs=[VMEM] * (len(groups) + 1),
-        out_specs=VMEM,
+    total, short_more = pl.pallas_call(
+        functools.partial(early_kernel, **place, unit=unit, work=works[3]),
+        out_shape=(jax.ShapeDtypeStruct((planes, half, depth), F32), shorts(works[3])),
+        in_specs=[VMEM] * (len(groups) + 6),
+        out_specs=(VMEM, VMEM),
         scratch_shapes=[pltpu.VMEM((planes * half, count), BF16)] * 2
-        + [pltpu.VMEM((depth, count), BF16)] * 2,
+        + [pltpu.VMEM((depth, count), BF16)] * 2
+        + planned,
         compiler_params=limit(12),
         cost_estimate=cost(2),
         name="early",
-    )(*groups, par)
+    )(*groups, par, plan, *own_tables)
     held = late.shape[0]
     rim = jax.ShapeDtypeStruct((RIM, half, depth), F32)
     packet = jax.ShapeDtypeStruct((RIM, half, depth), BF16)
@@ -751,11 +759,11 @@
     v_half, part = pl.pallas_call(
         functools.partial(kick_kernel, works=works),
         out_shape=(force, jax.ShapeDtypeStruct((8, CELL), F32)),
-        in_specs=[VMEM] * 7,
+        in_specs=[VMEM] * 8,
         out_specs=(VMEM, VMEM),
         compiler_params=limit(2),
         name="kick",
-    )(own, other, short_own, short_a, short_b, par, speed)
+    )(own, other, short_own, short_a, short_b, short_more, par, speed)
     if slabs == 4:
         parts = [part]
         for mask in (2, 3, 1):

time: 32 us -> 32 us (level)
    ppermute x3, waiting for transfers between devices: 1.1 us -> 0.64 us  [hop(): lax.ppermute(known, 'replica', [(i, i ^ mask) for i in range(members)])]
    pallas_call x1, Pallas kernels: 1.66 us -> 2.12 us  [local(): pl.pallas_call(functools.partial(early_kernel, **place, unit=unit, work=w...]
    pallas_call x1, Pallas kernels: 2.14 us -> 1.72 us  [local(): pl.pallas_call(functools.partial(force_kernel, **place, unit=unit, work=w...]
    ppermute x1, waiting for transfers between devices: 0.06 us -> 0.48 us  [local(): other = lax.ppermute(partner, 'replica', swap)]
where the time goes in v3:
time: 32 us; the launch traced here: 31.8 us
  starting transfers between devices  14.2 us (44%)
  Pallas kernels  13.8 us (43%)
  waiting for transfers between devices  2.29 us (7%)
  between operations  1.41 us (4%)
    ppermute x3, starting transfers between devices, hop(): lax.ppermute(known, 'replica', [(i, i ^ mask) for i in range(members)])  7.33 us
    pallas_call x1, Pallas kernels, local(): pl.pallas_call(functools.partial(middle_kernel, **place, members=members,...  3.09 us
    pallas_call x1, Pallas kernels, local(): pl.pallas_call(functools.partial(early_kernel, **place, unit=unit, work=w...  2.12 us
    pallas_call x1, Pallas kernels, local(): pl.pallas_call(functools.partial(own_kernel, unit=unit, cells=works[0]),...  1.88 us
    ppermute x3, starting transfers between devices, local(): lax.ppermute(part, 'brick', [(i, i ^ mask) for i in range(slabs)])  1.86 us
    ppermute x1, starting transfers between devices, local(): near_high = lax.ppermute(near_down, 'brick', back)  1.73 us
    pallas_call x1, Pallas kernels, local(): pl.pallas_call(functools.partial(force_kernel, **place, unit=unit, work=w...  1.72 us
    ppermute x1, starting transfers between devices, local(): got_y = lax.ppermute(packet_y, 'brick', route)  1.64 us
  transfers between devices with their start and end apart: 11, of which 4 were waited for; matrix products, arithmetic and copies ran while one was open for 0% of the time, Pallas kernels for 39%

profile of v3, /device:TPU:0, one launch (start us, length us, event | category | flops | bytes accessed | tf_op | source)
XLA Modules:
  0.0 31.8 jit_solution(8604237672254598843)
XLA Ops:
  0.6 4.1 %collective-permute-start = (f32[1,3,1,768]{3,2,1,0:T(1,128)}, f32[1,3,1,768]{3,2,1,0:T(1,128)S(1)}, u32[]{:S(2)}, u32[]{:S(2)}) collective-permute-start(f32[1,3,1,768]{3,2,1,0:T(1,128)} %bitcast.10), channel_id=1, source_target_pairs={{0,16},{4,20},{8,24},{12,28},{16,0},{20,4},{24,8},{28,12},{1,17},{... | collective-permute-start | bytes 27656 | tf_op jit(solution)/shard_map/ppermute | solution.py:557
  4.8 1.6 %prep.1 = (f32[1,3,1,768]{3,2,1,0:T(1,128)S(1)}, f32[3,1,768]{2,1,0:T(1,128)S(1)}, f32[8,768]{1,0:T(8,128)S(1)}, s32[2,8,128]{2,1,0:T(8,128)S(1)}, f32[17,16,128...) custom-call(f32[3,1,768]{2,1,0:T(1,128)} %bitcast.11, ...), custom_call_target="tpu_custom_call" | custom-call | flops 500000000 | bytes 1000000 | tf_op jit(solution)/shard_map/prep/pallas_call | solution.py:564
  6.4 0.1 collective-permute-start.5
  6.5 1.7 %collective-permute-start.6 = (f32[17,16,128]{2,1,0:T(8,128)S(1)}, f32[17,16,128]{2,1,0:T(8,128)S(1)}, u32[]{:S(2)}, u32[]{:S(2)}) collective-permute-start(f32[17,16,128]{2,1,0:T(8,128)S(1)} %get-tuple-element.61), channel_id=1, source_target_pairs={{1,0},{2,1},{3,2},{0,3},{5,4},{6,5},{7,6},{4,7},{9,8},{10,9},{11,1... | collective-permute-start | bytes 417800 | tf_op jit(solution)/shard_map/ppermute | solution.py:618
  8.2 0.0 collective-permute-done.refs_1_
  8.2 1.6 %collective-permute-start.1 = (f32[2,3,1,768]{3,2,1,0:T(1,128)S(1)}, f32[2,3,1,768]{3,2,1,0:T(1,128)S(1)}, u32[]{:S(2)}, u32[]{:S(2)}) collective-permute-start(f32[2,3,1,768]{3,2,1,0:T(1,128)S(1)} %pad_maximum_fusion.1), channel_id=1, source_target_pairs={{0,8},{4,12},{8,0},{12,4},{16,24},{20,28},{24,16},{28,20},{1,9},{5... | collective-permute-start | bytes 55304 | tf_op jit(solution)/shard_map/ppermute | solution.py:557
  9.9 1.9 %own_pairs.1 = (f32[768,128]{1,0:T(8,128)S(1)}, s32[768,128]{1,0:T(8,128)S(1)}, s32[768,128]{1,0:T(8,128)S(1)}, f32[768,128]{1,0:T(8,128)S(1)}, f32[3,512]{1,0:T(4,128)S(1)}) custom-call(f32[1,3,1,768]{3,2,1,0:T(1,128)S(1)} %get-tuple-element.43.mine.refs_0_.refs_5_, f32[8,768]{1,0:T(8,128)S(1)} %get-tuple-element.44.par.refs_3_.refs_4_, ...), custom_call_target="tpu_custom_call" | custom-call | flops 1000000000 | bytes 2000000 | tf_op jit(solution)/shard_map/own_pairs/pallas_call | solution.py:640
  11.8 0.3 collective-permute-done.1.refs_2_
  12.1 1.6 %collective-permute-start.2 = (f32[4,3,1,768]{3,2,1,0:T(1,128)S(1)}, f32[4,3,1,768]{3,2,1,0:T(1,128)S(1)}, u32[]{:S(2)}, u32[]{:S(2)}) collective-permute-start(f32[4,3,1,768]{3,2,1,0:T(1,128)S(1)} %pad_maximum_fusion), channel_id=1, source_target_pairs={{0,4},{4,0},{8,12},{12,8},{16,20},{20,16},{24,28},{28,24},{1,5},{5... | collective-permute-start | bytes 110600 | tf_op jit(solution)/shard_map/ppermute | solution.py:557
  13.6 2.1 %early.1 = (f32[14,64,128]{2,1,0:T(8,128)S(1)}, f32[3,128]{1,0:T(4,128)S(1)}) custom-call(f32[1,3,1,768]{3,2,1,0:T(1,128)S(1)} %get-tuple-element.43.mine.refs_0_.refs_5_, f32[1,3,1,768]{3,2,1,0:T(1,128)S(1)} %collective-permute-done.refs_1_, f32[2,3,1,768]{3,2,1,0:T(1,128)S(1)} %collective-permute-done.1.refs_2_, ...), custom_call_target="tpu_custom_call" | custom-call | flops 1000000000 | bytes 2000000 | tf_op jit(solution)/shard_map/early/pallas_call | solution.py:661
  15.8 0.3 %collective-permute-done.2.late = f32[4,3,1,768]{3,2,1,0:T(1,128)S(1)} collective-permute-done((f32[4,3,1,768]{3,2,1,0:T(1,128)S(1)}, f32[4,3,1,768]{3,2,1,0:T(1,128)S(1)}, u32[]{:S(2)}, u32[]{:S(2)}) %collective-permute-start.2) | collective-permute-done | bytes 36896 | tf_op jit(solution)/shard_map/ppermute | solution.py:557
  16.1 0.9 %across.1 = (f32[4,64,128]{2,1,0:T(8,128)S(1)}, bf16[4,64,128]{2,1,0:T(8,128)(2,1)S(1)}, f32[4,16,768]{2,1,0:T(8,128)S(1)}, f32[4,64,768]{2,1,0:T(8,128)S(1)}, bf16[4,128,768]{2,1,0:T(8,128)(2,1)S(1)}) custom-call(f32[4,3,1,768]{3,2,1,0:T(1,128)S(1)} %collective-permute-done.2.late, f32[8,768]{1,0:T(8,128)S(1)} %get-tuple-element.44.par.refs_3_.refs_4_, ...), custom_call_target="tpu_custom_call" | custom-call | flops 500000000 | bytes 1000000 | tf_op jit(solution)/shard_map/across/pallas_call | solution.py:676
  17.1 0.6 %beside.1 = (f32[4,64,128]{2,1,0:T(8,128)S(1)}, bf16[4,64,128]{2,1,0:T(8,128)(2,1)S(1)}) custom-call(f32[4,3,1,768]{3,2,1,0:T(1,128)S(1)} %collective-permute-done.2.late, f32[8,768]{1,0:T(8,128)S(1)} %get-tuple-element.44.par.refs_3_.refs_4_, f32[14,64,128]{2,1,0:T(8,128)S(1)} %get-tuple-element.50.total, f32[4,64,768]{2,1,0:T(8,128)S(1)} %get-tuple-element.53.y_in, ...), custom_call_target="tpu_custom_call" | custom-call | flops 500000000 | bytes 1000000 | tf_op jit(solution)/shard_map/beside/pallas_call | solution.py:694
  17.7 0.1 collective-permute-start.4
  17.7 1.6 %collective-permute-start.3 = (bf16[4,64,128]{2,1,0:T(8,128)(2,1)S(1)}, bf16[4,64,128]{2,1,0:T(8,128)(2,1)S(1)}, u32[]{:S(2)}, u32[]{:S(2)}) collective-permute-start(bf16[4,64,128]{2,1,0:T(8,128)(2,1)S(1)} %get-tuple-element.52), channel_id=1, source_target_pairs={{0,3},{1,2},{2,1},{3,0},{4,7},{5,6},{6,5},{7,4},{8,11},{9,10},{10,... | collective-permute-start | bytes 196616 | tf_op jit(solution)/shard_map/ppermute | solution.py:693
  19.4 0.0 collective-permute-done.5.low.near_low
  19.4 0.0 collective-permute-done.6.high.near_high
  19.4 0.3 %ghosts.1 = (f32[512,128]{1,0:T(8,128)S(1)}, s32[512,128]{1,0:T(8,128)S(1)}, s32[512,128]{1,0:T(8,128)S(1)}, f32[512,128]{1,0:T(8,128)S(1)}) custom-call(f32[17,16,128]{2,1,0:T(8,128)S(1)} %collective-permute-done.5.low.near_low, f32[17,16,128]{2,1,0:T(8,128)S(1)} %collective-permute-done.6.high.near_high), custom_call_target="tpu_custom_call" | custom-call | flops 500000000 | bytes 1000000 | tf_op jit(solution)/shard_map/ghosts/pallas_call | solution.py:650
  19.7 3.1 %middle.1 = (f32[6,64,128]{2,1,0:T(8,128)S(1)}, bf16[384,128]{1,0:T(8,128)(2,1)S(1)}, f32[3,768]{1,0:T(4,128)S(1)}, f32[3,512]{1,0:T(4,128)S(1)}) custom-call(f32[4,3,1,768]{3,2,1,0:T(1,128)S(1)} %collective-permute-done.2.late, f32[4,16,768]{2,1,0:T(8,128)S(1)} %get-tuple-element.57.x_in, f32[4,64,768]{2,1,0:T(8,128)S(1)} %get-tuple-element.53.y_in, ...), custom_call_target="tpu_custom_call" | custom-call | flops 1000000000 | bytes 2000000 | tf_op jit(solution)/shard_map/middle/pallas_call | solution.py:707
  22.8 0.0 collective-permute-done.4.got_c
  22.8 0.0 collective-permute-done.3.got_y
  22.8 0.8 %grad.1 = (f32[10,16,128]{2,1,0:T(8,128)S(1)}, bf16[896,128]{1,0:T(8,128)(2,1)S(1)}, f32[3,768]{1,0:T(4,128)S(1)}) custom-call(f32[4,3,1,768]{3,2,1,0:T(1,128)S(1)} %collective-permute-done.2.late, f32[8,768]{1,0:T(8,128)S(1)} %get-tuple-element.44.par.refs_3_.refs_4_, f32[4,64,128]{2,1,0:T(8,128)S(1)} %get-tuple-element.51.sent_y, ...), custom_call_target="tpu_custom_call" | custom-call | flops 500000000 | bytes 1000000 | tf_op jit(solution)/shard_map/grad/pallas_call | solution.py:722
  23.6 1.6 %collective-permute-start.7 = (f32[3,768]{1,0:T(4,128)S(1)}, f32[3,768]{1,0:T(4,128)S(1)}, u32[]{:S(2)}, u32[]{:S(2)}) collective-permute-start(f32[3,768]{1,0:T(4,128)S(1)} %get-tuple-element.72), channel_id=1, source_target_pairs={{0,4},{4,0},{8,12},{12,8},{16,20},{20,16},{24,28},{28,24},{1,5},{5... | collective-permute-start | bytes 27656 | tf_op jit(solution)/shard_map/ppermute | solution.py:744
  25.2 1.7 %force.1 = (f32[10,16,128]{2,1,0:T(8,128)}, f32[3,768]{1,0:T(4,128)S(1)}, f32[3,256]{1,0:T(4,128)S(1)}) custom-call(bf16[896,128]{1,0:T(8,128)(2,1)S(1)} %get-tuple-element.69.grad, f32[10,16,128]{2,1,0:T(8,128)S(1)} %get-tuple-element.70.deviation, f32[1,3,1,768]{3,2,1,0:T(1,128)S(1)} %get-tuple-element.43.mine.refs_0_.refs_5_, ...), custom_call_target="tpu_custom_call" | custom-call | flops 1000000000 | bytes 2000000 | tf_op jit(solution)/shard_map/force/pallas_call | solution.py:745
  26.9 0.5 %collective-permute-done.7.other = f32[3,768]{1,0:T(4,128)S(1)} collective-permute-done((f32[3,768]{1,0:T(4,128)S(1)}, f32[3,768]{1,0:T(4,128)S(1)}, u32[]{:S(2)}, u32[]{:S(2)}) %collective-permute-start.7) | collective-permute-done | bytes 9248 | tf_op jit(solution)/shard_map/ppermute | solution.py:744
  27.4 0.1 kick.1
  27.5 0.0 collective-permute-start.10
  27.5 0.3 %collective-permute-start.8 = (f32[8,128]{1,0:T(8,128)S(1)}, f32[8,128]{1,0:T(8,128)S(1)}, u32[]{:S(2)}, u32[]{:S(2)}) collective-permute-start(f32[8,128]{1,0:T(8,128)S(1)} %get-tuple-element.78.refs_0_), channel_id=1, source_target_pairs={{0,2},{1,3},{2,0},{3,1},{4,6},{5,7},{6,4},{7,5},{8,10},{9,11},{10,... | collective-permute-start | bytes 12296 | tf_op jit(solution)/shard_map/ppermute | solution.py:770
  27.8 1.5 %collective-permute-start.9 = (f32[8,128]{1,0:T(8,128)S(1)}, f32[8,128]{1,0:T(8,128)S(1)}, u32[]{:S(2)}, u32[]{:S(2)}) collective-permute-start(f32[8,128]{1,0:T(8,128)S(1)} %get-tuple-element.78.refs_0_), channel_id=1, source_target_pairs={{0,3},{1,2},{2,1},{3,0},{4,7},{5,6},{6,5},{7,4},{8,11},{9,10},{10,... | collective-permute-start | bytes 12296 | tf_op jit(solution)/shard_map/ppermute | solution.py:770
  30.0 0.0 collective-permute-done.10.refs_3_
  30.0 1.2 %collective-permute-done.8.refs_1_ = f32[8,128]{1,0:T(8,128)S(1)} collective-permute-done((f32[8,128]{1,0:T(8,128)S(1)}, f32[8,128]{1,0:T(8,128)S(1)}, u32[]{:S(2)}, u32[]{:S(2)}) %collective-permute-start.8) | collective-permute-done | bytes 4128 | tf_op jit(solution)/shard_map/ppermute | solution.py:770
  31.2 0.0 collective-permute-done.9.refs_2_
  31.2 0.6 %drift.1 = (f32[3,1,768]{2,1,0:T(1,128)}, f32[3,1,768]{2,1,0:T(1,128)}) custom-call(f32[8,128]{1,0:T(8,128)S(1)} %get-tuple-element.78.refs_0_, f32[8,128]{1,0:T(8,128)S(1)} %collective-permute-done.8.refs_1_, f32[8,128]{1,0:T(8,128)S(1)} %collective-permute-done.9.refs_2_, f32[8,128]{1,0:T(8,128)S(1)} %collective-permute-done.10.refs_3_, ...), custom_call_target="tpu_custom_call" | custom-call | tf_op jit(solution)/shard_map/drift/pallas_call | solution.py:774
  (2 shorter events, 0.1 us)
Async XLA Ops:
  0.6 7.6 %collective-permute-start = (f32[1,3,1,768]{3,2,1,0:T(1,128)}, f32[1,3,1,768]{3,2,1,0:T(1,128)S(1)}, u32[]{:S(2)}, u32[]{:S(2)}) collective-permute-start(f32[1,3,1,768]{3,2,1,0:T(1,128)} %bitcast.10), channel_id=1, source_target_pairs={{0,16},{4,20},{8,24},{12,28},{16,0},{20,4},{24,8},{28,12},{1,17},{... | collective-permute-start | bytes 27656 | tf_op jit(solution)/shard_map/ppermute | solution.py:557
  6.4 13.0 %collective-permute-start.5 = (f32[17,16,128]{2,1,0:T(8,128)S(1)}, f32[17,16,128]{2,1,0:T(8,128)S(1)}, u32[]{:S(2)}, u32[]{:S(2)}) collective-permute-start(f32[17,16,128]{2,1,0:T(8,128)S(1)} %get-tuple-element.60), channel_id=1, source_target_pairs={{0,1},{1,2},{2,3},{3,0},{4,5},{5,6},{6,7},{7,4},{8,9},{9,10},{10,1... | collective-permute-start | bytes 417800 | tf_op jit(solution)/shard_map/ppermute | solution.py:617
  6.5 12.9 %collective-permute-start.6 = (f32[17,16,128]{2,1,0:T(8,128)S(1)}, f32[17,16,128]{2,1,0:T(8,128)S(1)}, u32[]{:S(2)}, u32[]{:S(2)}) collective-permute-start(f32[17,16,128]{2,1,0:T(8,128)S(1)} %get-tuple-element.61), channel_id=1, source_target_pairs={{1,0},{2,1},{3,2},{0,3},{5,4},{6,5},{7,6},{4,7},{9,8},{10,9},{11,1... | collective-permute-start | bytes 417800 | tf_op jit(solution)/shard_map/ppermute | solution.py:618
  8.2 3.8 %collective-permute-start.1 = (f32[2,3,1,768]{3,2,1,0:T(1,128)S(1)}, f32[2,3,1,768]{3,2,1,0:T(1,128)S(1)}, u32[]{:S(2)}, u32[]{:S(2)}) collective-permute-start(f32[2,3,1,768]{3,2,1,0:T(1,128)S(1)} %pad_maximum_fusion.1), channel_id=1, source_target_pairs={{0,8},{4,12},{8,0},{12,4},{16,24},{20,28},{24,16},{28,20},{1,9},{5... | collective-permute-start | bytes 55304 | tf_op jit(solution)/shard_map/ppermute | solution.py:557
  12.1 4.0 %collective-permute-start.2 = (f32[4,3,1,768]{3,2,1,0:T(1,128)S(1)}, f32[4,3,1,768]{3,2,1,0:T(1,128)S(1)}, u32[]{:S(2)}, u32[]{:S(2)}) collective-permute-start(f32[4,3,1,768]{3,2,1,0:T(1,128)S(1)} %pad_maximum_fusion), channel_id=1, source_target_pairs={{0,4},{4,0},{8,12},{12,8},{16,20},{20,16},{24,28},{28,24},{1,5},{5... | collective-permute-start | bytes 110600 | tf_op jit(solution)/shard_map/ppermute | solution.py:557
  17.7 5.2 %collective-permute-start.4 = (bf16[4,64,128]{2,1,0:T(8,128)(2,1)S(1)}, bf16[4,64,128]{2,1,0:T(8,128)(2,1)S(1)}, u32[]{:S(2)}, u32[]{:S(2)}) collective-permute-start(bf16[4,64,128]{2,1,0:T(8,128)(2,1)S(1)} %get-tuple-element.56), channel_id=1, source_target_pairs={{0,1},{1,0},{2,3},{3,2},{4,5},{5,4},{6,7},{7,6},{8,9},{9,8},{10,11... | collective-permute-start | bytes 196616 | tf_op jit(solution)/shard_map/ppermute | solution.py:704
  17.7 5.1 %collective-permute-start.3 = (bf16[4,64,128]{2,1,0:T(8,128)(2,1)S(1)}, bf16[4,64,128]{2,1,0:T(8,128)(2,1)S(1)}, u32[]{:S(2)}, u32[]{:S(2)}) collective-permute-start(bf16[4,64,128]{2,1,0:T(8,128)(2,1)S(1)} %get-tuple-element.52), channel_id=1, source_target_pairs={{0,3},{1,2},{2,1},{3,0},{4,7},{5,6},{6,5},{7,4},{8,11},{9,10},{10,... | collective-permute-start | bytes 196616 | tf_op jit(solution)/shard_map/ppermute | solution.py:693
  23.6 3.8 %collective-permute-start.7 = (f32[3,768]{1,0:T(4,128)S(1)}, f32[3,768]{1,0:T(4,128)S(1)}, u32[]{:S(2)}, u32[]{:S(2)}) collective-permute-start(f32[3,768]{1,0:T(4,128)S(1)} %get-tuple-element.72), channel_id=1, source_target_pairs={{0,4},{4,0},{8,12},{12,8},{16,20},{20,16},{24,28},{28,24},{1,5},{5... | collective-permute-start | bytes 27656 | tf_op jit(solution)/shard_map/ppermute | solution.py:744
  27.5 2.5 %collective-permute-start.10 = (f32[8,128]{1,0:T(8,128)S(1)}, f32[8,128]{1,0:T(8,128)S(1)}, u32[]{:S(2)}, u32[]{:S(2)}) collective-permute-start(f32[8,128]{1,0:T(8,128)S(1)} %get-tuple-element.78.refs_0_), channel_id=1, source_target_pairs={{0,1},{1,0},{2,3},{3,2},{4,5},{5,4},{6,7},{7,6},{8,9},{9,8},{10,11... | collective-permute-start | bytes 12296 | tf_op jit(solution)/shard_map/ppermute | solution.py:770
  27.5 3.7 %collective-permute-start.8 = (f32[8,128]{1,0:T(8,128)S(1)}, f32[8,128]{1,0:T(8,128)S(1)}, u32[]{:S(2)}, u32[]{:S(2)}) collective-permute-start(f32[8,128]{1,0:T(8,128)S(1)} %get-tuple-element.78.refs_0_), channel_id=1, source_target_pairs={{0,2},{1,3},{2,0},{3,1},{4,6},{5,7},{6,4},{7,5},{8,10},{9,11},{10,... | collective-permute-start | bytes 12296 | tf_op jit(solution)/shard_map/ppermute | solution.py:770
  27.8 3.3 %collective-permute-start.9 = (f32[8,128]{1,0:T(8,128)S(1)}, f32[8,128]{1,0:T(8,128)S(1)}, u32[]{:S(2)}, u32[]{:S(2)}) collective-permute-start(f32[8,128]{1,0:T(8,128)S(1)} %get-tuple-element.78.refs_0_), channel_id=1, source_target_pairs={{0,3},{1,2},{2,1},{3,0},{4,7},{5,6},{6,5},{7,4},{8,11},{9,10},{10,... | collective-permute-start | bytes 12296 | tf_op jit(solution)/shard_map/ppermute | solution.py:770
